TPU v7x, 32 devices: a whole 2x2x4 slice. The times are simulated.
32 devices in a mesh: fsdp: 2 (over x), ctx: 4 (over z), tp: 4 (over y, core).
Axes of the slice: x: 2, y: 2, z: 4, core: 2. Of those that a mesh axis runs over, the one named last changes fastest.
Arguments:
- inputs: bfloat16 [2, 1024, 1024], P('fsdp', 'ctx'), may hold values from -6 to 6
- upstream: bfloat16 [2, 1024, 1024], P('fsdp', 'ctx'), may hold values from -6 to 6
- teacher: bfloat16 [2, 1024, 1024], P('fsdp', 'ctx'), may hold values from -8 to 8
- valid: int32 [2, 1024], P('fsdp', 'ctx'), may hold values from 0 to 1, as said below
- segment: int32 [2, 1024], P('fsdp', 'ctx'), may hold values from 0 to 7, never falling along the last dimension, each value on 1 to 512 neighbouring positions
- gain_one: float32 [1024], replicated, may hold values from 0.25 to 1.75
- query_weight: bfloat16 [1024, 1024], P('fsdp', 'tp'), may hold values from -0.1875 to 0.1875
- key_weight: bfloat16 [1024, 1024], P('fsdp', 'tp'), may hold values from -0.1875 to 0.1875
- value_weight: bfloat16 [1024, 1024], P('fsdp', 'tp'), may hold values from -0.1875 to 0.1875
- out_weight: bfloat16 [1024, 1024], P('tp', 'fsdp'), may hold values from -0.75 to 0.75
- gain_two: float32 [1024], replicated, may hold values from 0.25 to 1.75
- gate_weight: bfloat16 [1024, 2816], P('fsdp', 'tp'), may hold values from -0.1875 to 0.1875
- up_weight: bfloat16 [1024, 2816], P('fsdp', 'tp'), may hold values from -0.1875 to 0.1875
- down_weight: bfloat16 [2816, 1024], P('tp', 'fsdp'), may hold values from -0.21875 to 0.21875
Outputs:
- output: bfloat16 [2, 1024, 1024], P('fsdp', 'ctx')
- loss: float32 [2], replicated
- grad_inputs: float32 [2, 1024, 1024], P('fsdp', 'ctx')
- grad_gain_one: float32 [1024], P('fsdp')
- grad_query: float32 [1024, 1024], P('fsdp', 'tp')
- grad_key: float32 [1024, 1024], P('fsdp', 'tp')
- grad_value: float32 [1024, 1024], P('fsdp', 'tp')
- grad_out: float32 [1024, 1024], P('tp', 'fsdp')
- grad_gain_two: float32 [1024], P('fsdp')
- grad_gate: float32 [1024, 2816], P('fsdp', 'tp')
- grad_up: float32 [1024, 2816], P('fsdp', 'tp')
- grad_down: float32 [2816, 1024], P('tp', 'fsdp')
Inputs may be any that keep to these rules, and one draw needn't show every extreme that they name: `segment`: segment numbers never fall along a sequence; each document has 1 to 512 positions and one has exactly 512. The first token of every sequence is valid.
All inputs are finite; a program needn't handle non-finite values.
Results may differ from a plain program's by a relative error of at most 0.018.
Values may be sent and summed in bfloat16 or wider, within the bound.
A program may use at most 128 MiB of HBM per device.

v0:
```python
import jax
import jax.numpy as jnp
from jax import lax
from jax.sharding import PartitionSpec as P

HEAD_DIM = 64


def rms_scale(values_in, scales_in):
    return (
        values_in
        * lax.rsqrt(jnp.mean(values_in * values_in, axis=-1, keepdims=True) + 1e-05)
        * scales_in
    )


def swiglu(gate_act, up_act):
    return jax.nn.silu(gate_act) * up_act


def head_total(partial_sum):
    return lax.psum(partial_sum, "tp")


def contract(left, right, pattern):
    return jnp.einsum(pattern, left, right, preferred_element_type=jnp.float32)


def shards(
    inputs,
    upstream,
    teacher,
    valid,
    segment,
    gain_one,
    query_weight,
    key_weight,
    value_weight,
    out_weight,
    gain_two,
    gate_weight,
    up_weight,
    down_weight,
):
    seq_dev, ctx_tok, width = inputs.shape
    row_count = seq_dev * ctx_tok
    head_cols = query_weight.shape[1]
    heads_here = head_cols // HEAD_DIM
    scaling = HEAD_DIM ** (-0.5)
    full_query, full_key, full_value, full_gate, full_up = (
        lax.all_gather(query_weight, "fsdp", axis=0, tiled=True),
        lax.all_gather(key_weight, "fsdp", axis=0, tiled=True),
        lax.all_gather(value_weight, "fsdp", axis=0, tiled=True),
        lax.all_gather(gate_weight, "fsdp", axis=0, tiled=True),
        lax.all_gather(up_weight, "fsdp", axis=0, tiled=True),
    )
    full_out, full_down = (
        lax.all_gather(out_weight, "fsdp", axis=1, tiled=True),
        lax.all_gather(down_weight, "fsdp", axis=1, tiled=True),
    )
    seg_whole = lax.all_gather(segment, "ctx", axis=1, tiled=True)
    seq_len = seg_whole.shape[1]
    query_places = lax.axis_index("ctx") * ctx_tok + jnp.arange(ctx_tok, dtype=jnp.int32)
    key_places = jnp.arange(seq_len, dtype=jnp.int32)
    causal = key_places[None, :] <= query_places[:, None]
    flat_in = inputs.reshape(row_count, width).astype(jnp.float32)
    normed_one = rms_scale(flat_in, gain_one).astype(jnp.bfloat16)
    queries = jnp.dot(normed_one, full_query, preferred_element_type=jnp.float32).astype(
        jnp.bfloat16
    )
    keys_low = jnp.dot(normed_one, full_key, preferred_element_type=jnp.float32).astype(
        jnp.bfloat16
    )
    values_low = jnp.dot(normed_one, full_value, preferred_element_type=jnp.float32).astype(
        jnp.bfloat16
    )
    pairs = jnp.concatenate([keys_low, values_low], axis=1).reshape(seq_dev, ctx_tok, 2 * head_cols)
    pairs_all = lax.all_gather(pairs, "ctx", axis=1, tiled=True)
    query_heads = queries.reshape(seq_dev, ctx_tok, heads_here, HEAD_DIM)

    def scores_of(query_one, pairs_one, seg_all, seg_own):
        keys_one = pairs_one[:, :head_cols].reshape(seq_len, heads_here, HEAD_DIM)
        values_one = pairs_one[:, head_cols:].reshape(seq_len, heads_here, HEAD_DIM)
        allowed = causal & (seg_all[None, :] == seg_own[:, None])
        raw_scores = contract(query_one, keys_one, "qhd,khd->hqk") * scaling
        masked = jnp.where(allowed[None], raw_scores, -1e30)
        return (keys_one, values_one, allowed, masked)

    def attend_forward(bundle):
        query_one, pairs_one, seg_all, seg_own = bundle
        keys_one, values_one, allowed, masked = scores_of(query_one, pairs_one, seg_all, seg_own)
        top_score = jnp.max(masked, axis=-1, keepdims=True)
        exponent = jnp.where(allowed[None], jnp.exp(masked - top_score), 0.0)
        denominator = jnp.sum(exponent, axis=-1, keepdims=True)
        probs_low = (exponent / denominator).astype(jnp.bfloat16)
        mixed_one = contract(probs_low, values_one, "hqk,khd->qhd")
        return (mixed_one, top_score + jnp.log(denominator))

    mixed, log_norm = lax.map(attend_forward, (query_heads, pairs_all, seg_whole, segment))
    mixed_low = mixed.reshape(row_count, head_cols).astype(jnp.bfloat16)
    middle = flat_in + head_total(jnp.dot(mixed_low, full_out, preferred_element_type=jnp.float32))
    normed_two = rms_scale(middle, gain_two).astype(jnp.bfloat16)
    gate_low = jnp.dot(normed_two, full_gate, preferred_element_type=jnp.float32).astype(
        jnp.bfloat16
    )
    up_low = jnp.dot(normed_two, full_up, preferred_element_type=jnp.float32).astype(jnp.bfloat16)
    gate_wide = gate_low.astype(jnp.float32)
    up_wide = up_low.astype(jnp.float32)
    hidden_low = swiglu(gate_wide, up_wide).astype(jnp.bfloat16)
    result = middle + head_total(jnp.dot(hidden_low, full_down, preferred_element_type=jnp.float32))
    weighting = valid.reshape(row_count, 1).astype(jnp.float32)
    differ = result - teacher.reshape(row_count, width).astype(jnp.float32)
    per_sequence = jnp.sum((weighting * differ * differ).reshape(seq_dev, ctx_tok * width), axis=1)
    all_seqs = seq_dev * lax.axis_size("fsdp")
    own_seqs = lax.axis_index("fsdp") * seq_dev + jnp.arange(seq_dev, dtype=jnp.int32)
    placed = jnp.sum(
        jnp.where(
            own_seqs[:, None] == jnp.arange(all_seqs, dtype=jnp.int32)[None, :],
            per_sequence[:, None],
            0.0,
        ),
        axis=0,
    )
    counted, squared = lax.psum((jnp.sum(weighting), placed), ("fsdp", "ctx"))
    loss_value = squared * all_seqs / (counted * width)
    cotangent = upstream.reshape(row_count, width).astype(jnp.float32) + weighting * differ
    branch_grad = cotangent.astype(jnp.bfloat16)
    grad_down = contract(hidden_low, branch_grad, "rf,rd->fd")
    hidden_grad = contract(branch_grad, full_down, "rd,fd->rf")
    ignored, swiglu_back = jax.vjp(swiglu, gate_wide, up_wide)
    gate_grad, up_grad = swiglu_back(hidden_grad)
    gate_grad = gate_grad.astype(jnp.bfloat16)
    up_grad = up_grad.astype(jnp.bfloat16)
    grad_gate = contract(normed_two, gate_grad, "rd,rf->df")
    grad_up = contract(normed_two, up_grad, "rd,rf->df")
    norm_two_grad = head_total(
        contract(gate_grad, full_gate, "rf,df->rd") + contract(up_grad, full_up, "rf,df->rd")
    )
    ignored, norm_two_back = jax.vjp(rms_scale, middle, gain_two)
    middle_part, grad_gain_two = norm_two_back(norm_two_grad)
    middle_grad = cotangent + middle_part
    attn_grad = middle_grad.astype(jnp.bfloat16)
    grad_out = contract(mixed_low, attn_grad, "rh,rd->hd")
    mixed_grad = (
        contract(attn_grad, full_out, "rd,hd->rh")
        .astype(jnp.bfloat16)
        .reshape(seq_dev, ctx_tok, heads_here, HEAD_DIM)
    )

    def attend_backward(bundle):
        query_one, pairs_one, seg_all, seg_own, lse_one, grad_one = bundle
        keys_one, values_one, allowed, masked = scores_of(query_one, pairs_one, seg_all, seg_own)
        prob_full = jnp.where(allowed[None], jnp.exp(masked - lse_one), 0.0)
        value_grad = contract(prob_full.astype(jnp.bfloat16), grad_one, "hqk,qhd->khd")
        prob_grad = contract(grad_one, values_one, "qhd,khd->hqk")
        score_grad = (
            prob_full * (prob_grad - jnp.sum(prob_full * prob_grad, axis=-1, keepdims=True))
        ).astype(jnp.bfloat16)
        query_grad = contract(score_grad, keys_one, "hqk,khd->qhd") * scaling
        key_grad = contract(score_grad, query_one, "hqk,qhd->khd") * scaling
        return (
            query_grad,
            jnp.concatenate(
                [key_grad.reshape(seq_len, head_cols), value_grad.reshape(seq_len, head_cols)],
                axis=1,
            ),
        )

    query_grads, pair_terms = lax.map(
        attend_backward, (query_heads, pairs_all, seg_whole, segment, log_norm, mixed_grad)
    )
    pair_grads = (
        lax.psum_scatter(pair_terms, "ctx", scatter_dimension=1, tiled=True)
        .astype(jnp.bfloat16)
        .reshape(row_count, 2 * head_cols)
    )
    query_low = query_grads.reshape(row_count, head_cols).astype(jnp.bfloat16)
    key_low = pair_grads[:, :head_cols]
    value_low = pair_grads[:, head_cols:]
    grad_query = contract(normed_one, query_low, "rd,rh->dh")
    grad_key = contract(normed_one, key_low, "rd,rh->dh")
    grad_value = contract(normed_one, value_low, "rd,rh->dh")
    norm_one_grad = head_total(
        contract(query_low, full_query, "rh,dh->rd")
        + contract(key_low, full_key, "rh,dh->rd")
        + contract(value_low, full_value, "rh,dh->rd")
    )
    ignored, norm_one_back = jax.vjp(rms_scale, flat_in, gain_one)
    input_part, grad_gain_one = norm_one_back(norm_one_grad)
    grad_inputs = (middle_grad + input_part).reshape(seq_dev, ctx_tok, width)
    row_query, row_key, row_value, row_gate, row_up, row_one, row_two = (
        lax.psum_scatter(
            grad_query.astype(jnp.bfloat16), "fsdp", scatter_dimension=0, tiled=True
        ).astype(jnp.float32),
        lax.psum_scatter(
            grad_key.astype(jnp.bfloat16), "fsdp", scatter_dimension=0, tiled=True
        ).astype(jnp.float32),
        lax.psum_scatter(
            grad_value.astype(jnp.bfloat16), "fsdp", scatter_dimension=0, tiled=True
        ).astype(jnp.float32),
        lax.psum_scatter(
            grad_gate.astype(jnp.bfloat16), "fsdp", scatter_dimension=0, tiled=True
        ).astype(jnp.float32),
        lax.psum_scatter(
            grad_up.astype(jnp.bfloat16), "fsdp", scatter_dimension=0, tiled=True
        ).astype(jnp.float32),
        lax.psum_scatter(
            grad_gain_one.astype(jnp.bfloat16), "fsdp", scatter_dimension=0, tiled=True
        ).astype(jnp.float32),
        lax.psum_scatter(
            grad_gain_two.astype(jnp.bfloat16), "fsdp", scatter_dimension=0, tiled=True
        ).astype(jnp.float32),
    )
    col_out, col_down = (
        lax.psum_scatter(
            grad_out.astype(jnp.bfloat16), "fsdp", scatter_dimension=1, tiled=True
        ).astype(jnp.float32),
        lax.psum_scatter(
            grad_down.astype(jnp.bfloat16), "fsdp", scatter_dimension=1, tiled=True
        ).astype(jnp.float32),
    )
    sum_query, sum_key, sum_value, sum_gate, sum_up, sum_one, sum_two, sum_out, sum_down = (
        lax.psum(row_query.astype(jnp.bfloat16), "ctx").astype(jnp.float32),
        lax.psum(row_key.astype(jnp.bfloat16), "ctx").astype(jnp.float32),
        lax.psum(row_value.astype(jnp.bfloat16), "ctx").astype(jnp.float32),
        lax.psum(row_gate.astype(jnp.bfloat16), "ctx").astype(jnp.float32),
        lax.psum(row_up.astype(jnp.bfloat16), "ctx").astype(jnp.float32),
        lax.psum(row_one.astype(jnp.bfloat16), "ctx").astype(jnp.float32),
        lax.psum(row_two.astype(jnp.bfloat16), "ctx").astype(jnp.float32),
        lax.psum(col_out.astype(jnp.bfloat16), "ctx").astype(jnp.float32),
        lax.psum(col_down.astype(jnp.bfloat16), "ctx").astype(jnp.float32),
    )
    output = result.astype(jnp.bfloat16).reshape(seq_dev, ctx_tok, width)
    return (
        output,
        loss_value,
        grad_inputs,
        sum_one,
        sum_query,
        sum_key,
        sum_value,
        sum_out,
        sum_two,
        sum_gate,
        sum_up,
        sum_down,
    )


def solution(mesh):
    placed = (
        P("fsdp", "ctx", None),
        P("fsdp", "ctx", None),
        P("fsdp", "ctx", None),
        P("fsdp", "ctx"),
        P("fsdp", "ctx"),
        P(),
        P("fsdp", "tp"),
        P("fsdp", "tp"),
        P("fsdp", "tp"),
        P("tp", "fsdp"),
        P(),
        P("fsdp", "tp"),
        P("fsdp", "tp"),
        P("tp", "fsdp"),
    )
    return jax.shard_map(
        shards,
        mesh=mesh,
        in_specs=placed,
        out_specs=(
            P("fsdp", "ctx", None),
            P(),
            P("fsdp", "ctx", None),
            P("fsdp"),
            P("fsdp", "tp"),
            P("fsdp", "tp"),
            P("fsdp", "tp"),
            P("tp", "fsdp"),
            P("fsdp"),
            P("fsdp", "tp"),
            P("fsdp", "tp"),
            P("tp", "fsdp"),
        ),
        check_vma=False,
    )
```

profile of v0, /device:TPU:0, one launch (start us, length us, event | category | flops | bytes accessed | tf_op | source)
XLA Modules:
  0.0 628.7 jit_solution(3718089470991618106)
XLA Ops:
  8.1 1.3 fusion.18
  9.4 10.2 %all_gather.29 = bf16[1024,256]{1,0:T(8,128)(2,1)S(1)} all-gather(bf16[512,256]{1,0:T(8,128)(2,1)} %param.21), channel_id=1, replica_groups=mesh['fsdp'=2,'ctx'=4,'tp'=4] {'fsdp'}, dimensions={0}, use_global_device_ids=true | all-gather | bytes 786432 | tf_op jit(solution)/shard_map/all_gather | solution.py:52
  19.6 8.3 %all_gather.30 = bf16[1024,256]{1,0:T(8,128)(2,1)S(1)} all-gather(bf16[512,256]{1,0:T(8,128)(2,1)} %param.22), channel_id=1, replica_groups=mesh['fsdp'=2,'ctx'=4,'tp'=4] {'fsdp'}, dimensions={0}, use_global_device_ids=true | all-gather | bytes 786432 | tf_op jit(solution)/shard_map/all_gather | solution.py:53
  28.0 1.7 convolution_convert_fusion.12
  29.7 1.5 convolution_convert_fusion.11
  32.0 11.1 %all_gather.32 = s32[1,1024]{1,0:T(1,128)S(1)} all-gather(s32[1,256]{1,0:T(1,128)S(1)} %copy-done.47), channel_id=1, replica_groups=mesh['fsdp'=2,'ctx'=4,'tp'=4] {'ctx'}, dimensions={1}, use_global_device_ids=true | all-gather | bytes 5120 | tf_op jit(solution)/shard_map/all_gather | solution.py:61
  43.1 8.5 %all_gather.34 = bf16[1024,256]{1,0:T(8,128)(2,1)S(1)} all-gather(bf16[512,256]{1,0:T(8,128)(2,1)S(1)} %copy-done.34), channel_id=1, replica_groups=mesh['fsdp'=2,'ctx'=4,'tp'=4] {'fsdp'}, dimensions={0}, use_global_device_ids=true | all-gather | bytes 786432 | tf_op jit(solution)/shard_map/all_gather | solution.py:51
  51.5 7.0 %all_gather.35 = bf16[256,1024]{1,0:T(8,128)(2,1)S(1)} all-gather(bf16[256,512]{1,0:T(8,128)(2,1)S(1)} %copy-done.35), channel_id=1, replica_groups=mesh['fsdp'=2,'ctx'=4,'tp'=4] {'fsdp'}, dimensions={1}, use_global_device_ids=true | all-gather | bytes 786432 | tf_op jit(solution)/shard_map/all_gather | solution.py:58
  59.4 3.8 all-gather.12.cloned.1.call-done
  63.2 1.3 fusion.58
  65.2 1.0 fusion.1
  66.2 1.5 fusion
  68.3 1.8 fusion.15
  70.7 1.3 fusion.59
  73.9 33.0 %all-reduce.12.cloned.1.call-done = f32[256,1024]{1,0:T(8,128)} async-done(((f32[256,1024]{1,0:T(8,128)}), f32[256,1024]{1,0:T(8,128)}) %all-reduce.12.cloned.1.call-update) | async-done | bytes 1048592 | tf_op jit(solution)/shard_map/psum | solution.py:22
  106.8 1.5 multiply_reduce_fusion.3
  108.5 3.0 fusion.13
  111.5 13.5 %all-gather.8.cloned.1.call-done = bf16[1024,704]{0,1:T(8,128)(2,1)} async-done(((bf16[512,704]{0,1:T(8,128)(2,1)}), bf16[1024,704]{0,1:T(8,128)(2,1)}) %all-gather.8.cloned.1.call-update) | async-done | bytes 1441808 | tf_op jit(solution)/shard_map/all_gather | solution.py:55
  125.0 3.0 multiply_convert_fusion.3
  128.0 24.0 %all-gather.10.cloned.1.call-done = bf16[704,1024]{1,0:T(8,128)(2,1)} async-done(((bf16[704,512]{1,0:T(8,128)(2,1)}), bf16[704,1024]{1,0:T(8,128)(2,1)}) %all-gather.10.cloned.1.call-update) | async-done | bytes 1441808 | tf_op jit(solution)/shard_map/all_gather | solution.py:59
  152.0 2.9 fusion.60
  155.1 36.4 %all-reduce.14.cloned.1.call-done = f32[256,1024]{1,0:T(8,128)} async-done(((f32[256,1024]{1,0:T(8,128)}), f32[256,1024]{1,0:T(8,128)}) %all-reduce.14.cloned.1.call-update) | async-done | bytes 1048592 | tf_op jit(solution)/shard_map/psum | solution.py:22
  191.4 1.8 multiply_add_fusion
  193.5 2.3 multiply_convert_fusion.2
  196.7 1.6 convolution_add_fusion.2
  199.2 36.0 %all-reduce.16.cloned.1.call-done = f32[256,1024]{1,0:T(8,128)} async-done(((f32[256,1024]{1,0:T(8,128)}), f32[256,1024]{1,0:T(8,128)}) %all-reduce.16.cloned.1.call-update) | async-done | bytes 1048592 | tf_op jit(solution)/shard_map/psum | solution.py:22
  235.2 3.4 multiply_reduce_fusion.1
  239.3 1.5 fusion.23
  241.2 1.3 fusion.2
  242.5 1.9 multiply_reduce_fusion
  244.4 1.4 multiply_convert_fusion
  246.3 1.5 maximum_bitcast_fusion
  247.9 2.1 convolution_convert_fusion.3
  250.0 1.8 fusion.14
  252.5 2.3 convolution_convert_fusion.6
  254.9 2.9 convolution_convert_fusion.2
  257.9 1.6 convolution_convert_fusion
  259.6 1.6 convolution_convert_fusion.1
  261.4 30.8 %reduce-scatter.9.cloned.1.call-done = f32[1,256,512]{1,2,0:T(8,128)} async-done(((f32[1,1024,512]{1,2,0:T(8,128)}), f32[1,256,512]{1,2,0:T(8,128)}) %reduce-scatter.9.cloned.1.call-update) | async-done | bytes 524304 | tf_op jit(solution)/shard_map/reduce_scatter | solution.py:173
  292.1 1.1 convert_bitcast_fusion.2
  293.2 1.2 convolution_convert_fusion.5
  294.5 1.2 convolution_convert_fusion.4
  296.6 1.3 convolution_add_fusion
  298.0 10.0 %reduce-scatter.17.cloned.1.call-done = bf16[256,512]{1,0:T(8,128)(2,1)} async-done(((bf16[256,1024]{1,0:T(8,128)(2,1)}), bf16[256,512]{1,0:T(8,128)(2,1)}) %reduce-scatter.17.cloned.1.call-update) | async-done | bytes 262160 | tf_op jit(solution)/shard_map/reduce_scatter | solution.py:215
  308.1 17.5 %reduce-scatter.11.cloned.1.call-done = bf16[512,256]{1,0:T(8,128)(2,1)} async-done(((bf16[1024,256]{1,0:T(8,128)(2,1)}), bf16[512,256]{1,0:T(8,128)(2,1)}) %reduce-scatter.11.cloned.1.call-update) | async-done | bytes 262160 | tf_op jit(solution)/shard_map/reduce_scatter | solution.py:192
  325.6 27.6 %reduce-scatter.23.cloned.1.call-done = bf16[704,512]{1,0:T(8,128)(2,1)} async-done(((bf16[704,1024]{1,0:T(8,128)(2,1)}), bf16[704,512]{1,0:T(8,128)(2,1)}) %reduce-scatter.23.cloned.1.call-update) | async-done | bytes 720912 | tf_op jit(solution)/shard_map/reduce_scatter | solution.py:218
  353.1 27.6 %reduce-scatter.21.cloned.1.call-done = bf16[512,704]{0,1:T(8,128)(2,1)} async-done(((bf16[1024,704]{0,1:T(8,128)(2,1)}), bf16[512,704]{0,1:T(8,128)(2,1)}) %reduce-scatter.21.cloned.1.call-update) | async-done | bytes 720912 | tf_op jit(solution)/shard_map/reduce_scatter | solution.py:204
  380.7 27.4 %reduce-scatter.19.cloned.1.call-done = bf16[512,704]{0,1:T(8,128)(2,1)} async-done(((bf16[1024,704]{0,1:T(8,128)(2,1)}), bf16[512,704]{0,1:T(8,128)(2,1)}) %reduce-scatter.19.cloned.1.call-update) | async-done | bytes 720912 | tf_op jit(solution)/shard_map/reduce_scatter | solution.py:201
  408.1 17.5 %reduce-scatter.13.cloned.1.call-done = bf16[512,256]{1,0:T(8,128)(2,1)} async-done(((bf16[1024,256]{1,0:T(8,128)(2,1)}), bf16[512,256]{1,0:T(8,128)(2,1)}) %reduce-scatter.13.cloned.1.call-update) | async-done | bytes 262160 | tf_op jit(solution)/shard_map/reduce_scatter | solution.py:195
  425.6 17.3 %reduce-scatter.15.cloned.1.call-done = bf16[512,256]{1,0:T(8,128)(2,1)} async-done(((bf16[1024,256]{1,0:T(8,128)(2,1)}), bf16[512,256]{1,0:T(8,128)(2,1)}) %reduce-scatter.15.cloned.1.call-update) | async-done | bytes 262160 | tf_op jit(solution)/shard_map/reduce_scatter | solution.py:198
  445.5 21.2 %all-reduce.2 = (f32[2]{0:T(128)S(1)}, f32[]{:T(128)}) all-reduce(f32[2]{0:T(128)S(1)} %compare_select_fusion, f32[]{:T(128)} %convert_reduce_fusion), channel_id=1, replica_groups=mesh['fsdp'=2,'ctx'=4,'tp'=4] {'fsdp','ctx'}, use_global_device_ids=true, to_apply=%region_7.8 | all-reduce | flops 3 | bytes 24 | tf_op jit(solution)/shard_map/psum | solution.py:124
  467.8 14.4 %all-reduce.18.cloned.1.call-done = f32[256,1024]{1,0:T(8,128)} async-done(((f32[256,1024]{1,0:T(8,128)}), f32[256,1024]{1,0:T(8,128)}) %all-reduce.18.cloned.1.call-update) | async-done | bytes 1048592 | tf_op jit(solution)/shard_map/psum | solution.py:22
  482.2 1.6 fusion.17
  483.8 4.9 all-reduce.5
  488.9 12.3 %all-reduce.3 = (bf16[512]{0:T(512)(128)(2,1)S(1)}, bf16[512]{0:T(512)(128)(2,1)S(1)}) all-reduce(bf16[512]{0:T(512)(128)(2,1)S(1)} %dynamic-slice.2, bf16[512]{0:T(512)(128)(2,1)S(1)} %dynamic-slice.4), channel_id=1, replica_groups=mesh['fsdp'=2,'ctx'=4,'tp'=4] {'ctx'}, use_global_device_ids=true, to_apply=%region_18.19 | all-reduce | flops 1024 | bytes 4096 | tf_op jit(solution)/shard_map/psum | solution.py:228
  502.3 2.5 fusion.25
  504.8 104.2 %all-reduce.20.cloned.1.call-done = (bf16[512,256]{1,0:T(8,128)(2,1)}, bf16[512,256]{1,0:T(8,128)(2,1)}, bf16[512,256]{1,0:T(8,128)(2,1)}, bf16[256,512]{1,0:T(8...) async-done(((bf16[512,256]{1,0:T(8,128)(2,1)}, bf16[512,256]{1,0:T(8,128)(2,1)}, bf16[512,256]{1,0:T(8,128)(2,1)}, ...) | async-done | bytes 3211280 | tf_op jit(solution)/shard_map/psum | solution.py:223
  609.1 1.9 convert_element_type.237
  610.9 1.8 convert_element_type.239
  612.7 1.8 convert_element_type.241
  614.5 1.8 convert_element_type.243
  616.3 2.4 convert_element_type.247
  618.7 1.3 convert_element_type.249
  620.0 1.3 convert_element_type.251
  (163 shorter events, 14.8 us)
Async XLA Ops:
  8.0 50.9 %copy-start.3 = (bf16[1,256,1024]{2,1,0:T(8,128)(2,1)S(1)}, bf16[1,256,1024]{2,1,0:T(8,128)(2,1)}, u32[]{:S(2)}) copy-start(bf16[1,256,1024]{2,1,0:T(8,128)(2,1)} %param.14) | copy-start | bytes 1572868
  8.0 50.9 %copy-start.37 = (f32[1024]{0:T(1024)S(1)}, f32[1024]{0:T(1024)}, u32[]{:S(2)}) copy-start(f32[1024]{0:T(1024)} %param.19) | copy-start | bytes 12292
  8.0 23.9 %copy-start.47 = (s32[1,256]{1,0:T(1,128)S(1)}, s32[1,256]{1,0:T(1,128)}, u32[]{:S(2)}) copy-start(s32[1,256]{1,0:T(1,128)} %param.18) | copy-start | bytes 3076
  8.0 35.0 %copy-start.34 = (bf16[512,256]{1,0:T(8,128)(2,1)S(1)}, bf16[512,256]{1,0:T(8,128)(2,1)}, u32[]{:S(2)}) copy-start(bf16[512,256]{1,0:T(8,128)(2,1)} %param.20) | copy-start | bytes 786436
  8.1 43.5 %copy-start.35 = (bf16[256,512]{1,0:T(8,128)(2,1)S(1)}, bf16[256,512]{1,0:T(8,128)(2,1)}, u32[]{:S(2)}) copy-start(bf16[256,512]{1,0:T(8,128)(2,1)} %param.23) | copy-start | bytes 786436
  8.1 55.1 %all-gather.12.cloned.1.call-start = ((), (), s32[]{:S(2)}) async-start(), calls=%async_computation.23 | async-start | bytes 1310720 | tf_op jit(solution)/shard_map/all_gather | solution.py:78
  9.4 22.6 %copy-start.41 = (f32[256]{0:T(256)}, f32[256]{0:T(256)S(1)}, u32[]{:S(2)}) copy-start(f32[256]{0:T(256)S(1)} %fusion.18) | copy-start | bytes 3076
  9.4 49.9 %copy-start.44 = (f32[256]{0:T(256)}, f32[256]{0:T(256)S(1)}, u32[]{:S(2)}) copy-start(f32[256]{0:T(256)S(1)} %fusion.44) | copy-start | bytes 3076
  19.6 8.3 %copy-start.17 = (bf16[1024,256]{1,0:T(8,128)(2,1)}, bf16[1024,256]{1,0:T(8,128)(2,1)S(1)}, u32[]{:S(2)}) copy-start(bf16[1024,256]{1,0:T(8,128)(2,1)S(1)} %all_gather.29) | copy-start | bytes 1572868
  28.0 15.1 %copy-start.15 = (bf16[1024,256]{1,0:T(8,128)(2,1)}, bf16[1024,256]{1,0:T(8,128)(2,1)S(1)}, u32[]{:S(2)}) copy-start(bf16[1024,256]{1,0:T(8,128)(2,1)S(1)} %all_gather.30) | copy-start | bytes 1572868
  31.9 74.9 %all-reduce.12.cloned.1.call-start = ((), (), s32[]{:S(2)}) async-start(), calls=%async_computation.8 | async-start | bytes 2097152 | tf_op jit(solution)/shard_map/psum | solution.py:22
  51.5 7.3 %copy-start.13 = (bf16[1024,256]{1,0:T(8,128)(2,1)}, bf16[1024,256]{1,0:T(8,128)(2,1)S(1)}, u32[]{:S(2)}) copy-start(bf16[1024,256]{1,0:T(8,128)(2,1)S(1)} %all_gather.34) | copy-start | bytes 1572868
  58.6 11.5 %copy-start.8 = (bf16[256,1024]{1,0:T(8,128)(2,1)}, bf16[256,1024]{1,0:T(8,128)(2,1)S(1)}, u32[]{:S(2)}) copy-start(bf16[256,1024]{1,0:T(8,128)(2,1)S(1)} %all_gather.35) | copy-start | bytes 1572868
  64.4 3.3 copy-start.29
  66.2 3.9 copy-start
  70.1 38.2 %copy-start.36 = (f32[1024]{0:T(1024)S(1)}, f32[1024]{0:T(1024)}, u32[]{:S(2)}) copy-start(f32[1024]{0:T(1024)} %param.24) | copy-start | bytes 12292
  72.1 36.5 %all-gather.6.cloned.1.call-start = ((), (), s32[]{:S(2)}) async-start(), calls=%async_computation.9 | async-start | bytes 2162688 | tf_op jit(solution)/shard_map/all_gather | solution.py:54
  72.6 52.4 %all-gather.8.cloned.1.call-start = ((), (), s32[]{:S(2)}) async-start(), calls=%async_computation.10 | async-start | bytes 2162688 | tf_op jit(solution)/shard_map/all_gather | solution.py:55
  73.2 78.8 %all-gather.10.cloned.1.call-start = ((), (), s32[]{:S(2)}) async-start(), calls=%async_computation.11 | async-start | bytes 2162688 | tf_op jit(solution)/shard_map/all_gather | solution.py:59
  73.8 117.6 %all-reduce.14.cloned.1.call-start = ((), (), s32[]{:S(2)}) async-start(), calls=%async_computation.12 | async-start | bytes 2097152 | tf_op jit(solution)/shard_map/psum | solution.py:22
  108.3 19.7 %copy-start.43 = (f32[256]{0:T(256)}, f32[256]{0:T(256)S(1)}, u32[]{:S(2)}) copy-start(f32[256]{0:T(256)S(1)} %get-tuple-element.84) | copy-start | bytes 3076
  108.5 46.5 %copy-start.5 = (bf16[256,1024]{1,0:T(8,128)(2,1)}, bf16[256,1024]{1,0:T(8,128)(2,1)S(1)}, u32[]{:S(2)}) copy-start(bf16[256,1024]{1,0:T(8,128)(2,1)S(1)} %multiply_convert_fusion.1) | copy-start | bytes 1572868
  111.5 43.5 %copy-start.48 = (s32[1,256]{1,0:T(1,128)S(1)}, s32[1,256]{1,0:T(1,128)}, u32[]{:S(2)}) copy-start(s32[1,256]{1,0:T(1,128)} %param.17) | copy-start | bytes 3076
  111.5 79.9 %copy-start.12 = (bf16[1,256,1024]{2,1,0:T(8,128)(2,1)S(1)}, bf16[1,256,1024]{2,1,0:T(8,128)(2,1)}, u32[]{:S(2)}) copy-start(bf16[1,256,1024]{2,1,0:T(8,128)(2,1)} %param.16) | copy-start | bytes 1572868
  128.0 63.5 %copy-start.23 = (bf16[256,704]{0,1:T(8,128)(2,1)}, bf16[256,704]{0,1:T(8,128)(2,1)S(1)}, u32[]{:S(2)}) copy-start(bf16[256,704]{0,1:T(8,128)(2,1)S(1)} %get-tuple-element.93) | copy-start | bytes 1081348
  155.0 80.2 %all-reduce.16.cloned.1.call-start = ((), (), s32[]{:S(2)}) async-start(), calls=%async_computation.13 | async-start | bytes 2097152 | tf_op jit(solution)/shard_map/psum | solution.py:22
  155.1 40.8 %copy-start.40 = (f32[1,256]{1,0:T(1,128)}, f32[1,256]{1,0:T(1,128)S(1)}, u32[]{:S(2)}) copy-start(f32[1,256]{1,0:T(1,128)S(1)} %convert_element_type.214) | copy-start | bytes 3076
  191.4 1.8 copy-start.21
  191.4 2.0 copy-start.51
  193.2 46.0 %copy-start.2 = (f32[256,1024]{1,0:T(8,128)}, f32[256,1024]{1,0:T(8,128)S(1)}, u32[]{:S(2)}) copy-start(f32[256,1024]{1,0:T(8,128)S(1)} %multiply_add_fusion) | copy-start | bytes 3145732
  193.2 2.6 copy-start.7
  193.5 3.2 copy-start.22
  195.8 0.8 copy-start.25
  195.8 39.3 %copy-start.11 = (f32[256,1024]{1,0:T(8,128)S(1)}, f32[256,1024]{1,0:T(8,128)}, u32[]{:S(2)}) copy-start(f32[256,1024]{1,0:T(8,128)} %all-reduce.14.cloned.1.call-done) | copy-start | bytes 3145732
  198.3 93.8 %reduce-scatter.9.cloned.1.call-start = ((), (), s32[]{:S(2)}) async-start(), calls=%async_computation.14 | async-start | bytes 2621440 | tf_op jit(solution)/shard_map/reduce_scatter | solution.py:173
  235.2 5.6 copy-start.9
  235.2 6.0 copy-start.1
  241.1 1.3 copy-start.30
  247.8 4.7 copy-start.38
  247.8 4.7 copy-start.45
  247.8 7.0 %copy-start.24 = (bf16[256,704]{0,1:T(8,128)(2,1)S(1)}, bf16[256,704]{0,1:T(8,128)(2,1)}, u32[]{:S(2)}) copy-start(bf16[256,704]{0,1:T(8,128)(2,1)} %copy-done.23) | copy-start | bytes 1081348
  247.9 60.2 %reduce-scatter.17.cloned.1.call-start = ((), (), s32[]{:S(2)}) async-start(), calls=%async_computation.19 | async-start | bytes 786432 | tf_op jit(solution)/shard_map/reduce_scatter | solution.py:215
  250.0 75.6 %reduce-scatter.11.cloned.1.call-start = ((), (), s32[]{:S(2)}) async-start(), calls=%async_computation.16 | async-start | bytes 786432 | tf_op jit(solution)/shard_map/reduce_scatter | solution.py:192
  251.8 6.0 copy-start.6
  251.9 6.0 copy-start.26
  254.8 4.9 copy-start.20
  254.8 98.3 %reduce-scatter.23.cloned.1.call-start = ((), (), s32[]{:S(2)}) async-start(), calls=%async_computation.22 | async-start | bytes 2162688 | tf_op jit(solution)/shard_map/reduce_scatter | solution.py:218
  257.8 35.4 %copy-start.4 = (bf16[1,256,1024]{2,1,0:T(8,128)(2,1)S(1)}, bf16[1,256,1024]{2,1,0:T(8,128)(2,1)}, u32[]{:S(2)}) copy-start(bf16[1,256,1024]{2,1,0:T(8,128)(2,1)} %param.14) | copy-start | bytes 1572868
  257.8 122.8 %reduce-scatter.21.cloned.1.call-start = ((), (), s32[]{:S(2)}) async-start(), calls=%async_computation.21 | async-start | bytes 2162688 | tf_op jit(solution)/shard_map/reduce_scatter | solution.py:204
  259.6 36.3 %copy-start.14 = (bf16[1024,256]{1,0:T(8,128)(2,1)S(1)}, bf16[1024,256]{1,0:T(8,128)(2,1)}, u32[]{:S(2)}) copy-start(bf16[1024,256]{1,0:T(8,128)(2,1)} %copy-done.13) | copy-start | bytes 1572868
  259.6 36.3 %copy-start.33 = (bf16[4,64,256]{2,1,0:T(8,128)(2,1)S(1)}, bf16[4,64,256]{2,1,0:T(8,128)(2,1)}, u32[]{:S(2)}) copy-start(bf16[4,64,256]{2,1,0:T(8,128)(2,1)} %copy-done.32) | copy-start | bytes 393220
  259.6 148.5 %reduce-scatter.19.cloned.1.call-start = ((), (), s32[]{:S(2)}) async-start(), calls=%async_computation.20 | async-start | bytes 2162688 | tf_op jit(solution)/shard_map/reduce_scatter | solution.py:201
  261.3 34.9 %copy-start.18 = (bf16[1024,256]{1,0:T(8,128)(2,1)S(1)}, bf16[1024,256]{1,0:T(8,128)(2,1)}, u32[]{:S(2)}) copy-start(bf16[1024,256]{1,0:T(8,128)(2,1)} %copy-done.17) | copy-start | bytes 1572868
  261.3 164.3 %reduce-scatter.13.cloned.1.call-start = ((), (), s32[]{:S(2)}) async-start(), calls=%async_computation.17 | async-start | bytes 786432 | tf_op jit(solution)/shard_map/reduce_scatter | solution.py:195
  293.2 3.4 copy-start.16
  294.5 148.4 %reduce-scatter.15.cloned.1.call-start = ((), (), s32[]{:S(2)}) async-start(), calls=%async_computation.18 | async-start | bytes 786432 | tf_op jit(solution)/shard_map/reduce_scatter | solution.py:198
  295.8 186.4 %all-reduce.18.cloned.1.call-start = ((), (), s32[]{:S(2)}) async-start(), calls=%async_computation.15 | async-start | bytes 2097152 | tf_op jit(solution)/shard_map/psum | solution.py:22
  296.6 146.4 %copy-start.50 = (u32[32]{0:T(128)S(1)}, u32[32]{0:T(128)}, u32[]{:S(2)}) copy-start(u32[32]{0:T(128)} %constant.94) | copy-start | bytes 388
  296.6 146.9 %copy-start.49 = (s32[1,256]{1,0:T(1,128)S(1)}, s32[1,256]{1,0:T(1,128)}, u32[]{:S(2)}) copy-start(s32[1,256]{1,0:T(1,128)} %param.17) | copy-start | bytes 3076
  296.6 187.2 %copy-start.46 = (bf16[1024]{0:T(1024)(128)(2,1)S(1)}, bf16[1024]{0:T(1024)(128)(2,1)}, u32[]{:S(2)}) copy-start(bf16[1024]{0:T(1024)(128)(2,1)} %get-tuple-element.56) | copy-start | bytes 6148
  296.6 205.7 %copy-start.42 = (f32[256]{0:T(256)S(1)}, f32[256]{0:T(256)}, u32[]{:S(2)}) copy-start(f32[256]{0:T(256)} %copy-done.41) | copy-start | bytes 3076
  298.0 311.1 %all-reduce.20.cloned.1.call-start = ((), (), s32[]{:S(2)}) async-start(), calls=%async_computation.24 | async-start | bytes 6422528 | tf_op jit(solution)/shard_map/psum | solution.py:223
  609.1 9.7 %copy-start.28 = (bf16[512,704]{0,1:T(8,128)(2,1)S(1)}, bf16[512,704]{0,1:T(8,128)(2,1)}, u32[]{:S(2)}) copy-start(bf16[512,704]{0,1:T(8,128)(2,1)} %get-tuple-element.80) | copy-start | bytes 2162692
  609.1 11.0 %copy-start.27 = (bf16[704,512]{1,0:T(8,128)(2,1)S(1)}, bf16[704,512]{1,0:T(8,128)(2,1)}, u32[]{:S(2)}) copy-start(bf16[704,512]{1,0:T(8,128)(2,1)} %get-tuple-element.81) | copy-start | bytes 2162692
  (5 other events, 3.4 us)
Sparse Core Ops, SparseCore 0:
  32.0 31.0 all-gather.11
  72.2 34.5 all-reduce.11
  155.1 36.2 all-reduce.13
  198.4 36.7 all-reduce.15
  248.0 44.0 reduce-scatter.8
  294.2 13.8 reduce-scatter.16
  310.9 14.6 reduce-scatter.10
  328.4 24.6 reduce-scatter.22
  355.9 24.6 reduce-scatter.20
  383.3 24.6 reduce-scatter.18
  410.9 14.6 reduce-scatter.12
  428.2 14.6 reduce-scatter.14
  445.9 36.3 all-reduce.17
  485.0 124.0 all-reduce.19
Sparse Core Ops, SparseCore 1:
  74.1 23.8 all-gather.5
  99.4 25.5 all-gather.7
  126.4 25.5 all-gather.9
where the time goes:
time: 630 us; the launch traced here: 629 us
  waiting for transfers between devices  443 us (70%)
  blocking collectives  83.5 us (13%)
  matrix products  42 us (7%)
  other arithmetic  36.8 us (6%)
  between operations  17.6 us (3%)
    psum x4, waiting for transfers between devices, head_total(): return lax.psum(partial_sum, 'tp')  120 us
    psum x1, waiting for transfers between devices, shards(): lax.psum(row_query.astype(jnp.bfloat16), 'ctx').astype(jnp.float32)  104 us
    reduce_scatter x1, waiting for transfers between devices, shards(): lax.psum_scatter(pair_terms, 'ctx', scatter_dimension=1, tiled=True)  30.8 us
    dot_general x20, matrix products, contract(): return jnp.einsum(pattern, left, right, preferred_element_type=jnp.float32)  28.2 us
    reduce_scatter x1, waiting for transfers between devices, shards(): lax.psum_scatter(grad_up.astype(jnp.bfloat16), 'fsdp', scatter_dimension=...  27.6 us
    reduce_scatter x1, waiting for transfers between devices, shards(): lax.psum_scatter(grad_down.astype(jnp.bfloat16), 'fsdp', scatter_dimensio...  27.6 us
    reduce_scatter x1, waiting for transfers between devices, shards(): lax.psum_scatter(grad_gate.astype(jnp.bfloat16), 'fsdp', scatter_dimensio...  27.4 us
    all_gather x1, waiting for transfers between devices, shards(): lax.all_gather(down_weight, 'fsdp', axis=1, tiled=True)  24 us
  transfers between devices with their start and end apart: 17, of which 16 were waited for; matrix products, arithmetic and copies ran while one was open for 6% of the time, Pallas kernels for 0%

commit v1 on v0

v1 whole, which is shorter than its diff:
```python
import functools
from types import SimpleNamespace

import jax
import jax.numpy as jnp
from jax import lax
from jax.experimental import pallas as pl
from jax.experimental.pallas import tpu as pltpu
from jax.sharding import PartitionSpec as P

HEAD_DIM = 64
EPS = 1e-05
MESH = pl.DeviceIdType.MESH
NCHK = 4
SKEW = 3
f32, bf16 = jnp.float32, jnp.bfloat16


class Plan:
    def __init__(self, fsdp, ctx, rows, width, head_cols, hidden, seq_len):
        self.F, self.C, self.R, self.D = fsdp, ctx, rows, width
        self.HC, self.FF = head_cols, hidden
        self.DF = width // fsdp
        self.W = -(-(seq_len // 2 - 1) // rows)
        self.N = 3 * hidden + 4 * head_cols
        self.CH = next(
            k for k in range(16, self.N + 1, 16) if self.N % k == 0 and k * self.DF >= 32768
        )
        self.NCH = self.N // self.CH
        self.base, self.total = SimpleNamespace(), 0
        peers = fsdp - 1
        for name, count in dict(
            xz=self.W, sg=self.W, xc=self.W, wd=10 * peers, wr=10 * peers,
            a=3 * NCHK, b=3 * NCHK, n2=NCHK, yb=1, dy=NCHK, dh=NCHK,
            lc=1, lr=ctx, ll=ctx, lx=peers, d1=self.W + 1, d2=self.W + 1, dz=self.W + 1,
            g1=1, g2=1, i1=1, i2=1, i3=1, gx=peers * (self.NCH + 1),
            zin=self.NCH + 1, zmid=self.NCH + 1, zout=self.NCH + 1,
        ).items():
            setattr(self.base, name, self.total)
            self.total += count


def contract(left, right, dims):
    return lax.dot_general(left, right, ((dims[:1], dims[1:]), ((), ())), preferred_element_type=f32)


def total_of(v):
    return jnp.sum(jnp.sum(v, axis=1, keepdims=True), axis=0, keepdims=True)


def scratch_of(p):
    R, D, HC, FF, DF, F, C, W = p.R, p.D, p.HC, p.FF, p.DF, p.F, p.C, p.W
    HF, Q, KR, H = R // 2, R // 4, (p.W + 1) * p.R, p.HC // HEAD_DIM
    NG = p.N + 16
    return dict(
        XB=((KR, D), bf16), SG=((W + 1, 1, R), jnp.int32), N1=((KR, D), bf16),
        WQKV=((D, 3 * HC), bf16), WO=((HC, D), bf16), WG=((D, FF), bf16),
        WU=((D, FF), bf16), WD=((FF, D), bf16),
        QB=((R, HC), bf16), KB=((KR, HC), bf16), VB=((KR, HC), bf16),
        PM=((H, R, KR), f32), S=((R, KR), f32), PB=((R, KR), bf16), DSB=((R, KR), bf16),
        BIAS=((R, KR), f32), O32=((R, HC), f32), DK32=((KR, HC), f32), DV32=((KR, HC), f32),
        OB=((R, HC), bf16), DOB=((R, HC), bf16), VC=((R, 128), f32),
        H=((HF, D), f32), DY=((HF, D), f32), DH=((HF, D), f32), P32=((HF, D), f32),
        UP=((HF, D), bf16), TE=((HF, D), bf16),
        N2=((R, D), bf16), DYB=((R, D), bf16), DHB=((R, D), bf16),
        GB=((R, FF), bf16), UB=((R, FF), bf16), AB=((R, FF), bf16),
        DGB=((R, FF), bf16), DUB=((R, FF), bf16), DA32=((R, FF), f32),
        DALL=((KR, 3 * HC), bf16),
        D1S=((W + 1, HF, D), bf16), D1R=((W + 1, HF, D), bf16), D1O=((W + 1, HF, D), f32),
        D2S=((W + 1, Q, D), bf16), D2R=((W + 1, Q, D), bf16), DZR=((W + 1, Q, D), bf16),
        DZS=((W + 1, Q, D), bf16),
        GT=((3, 8, D), f32), GR=((2, 8, D), f32),
        LT=((2, 8, 128), f32), LB=((C, 8, 128), f32), LX=((F, C, 8, 128), f32),
        XS=((F, NG, DF), bf16), XR=((F - 1, NG, DF), bf16), SI=((NG, DF), bf16),
        ZO=((NG, DF), bf16), ZI=((NG, DF), bf16),
        S1=((3, HF, D), bf16), R1=((3, HF, D), bf16), S2=((3, HF, D), bf16), R2=((3, HF, D), bf16),
    )


def layer_kernel(p, names, *refs):
    v = SimpleNamespace(**dict(zip(names, refs[18:], strict=False)))
    (
        v.x, v.upstream, v.teacher, v.valid, v.segment, v.gain_one, v.wq, v.wk, v.wv, v.wo,
        v.gain_two, v.wg, v.wu, v.wd, v.GRAD, v.GIB, v.YB, v.LOSS,
    ) = refs[:18]
    ss, rs, ls = refs[-3:]
    R, D, HC, FF, DF, F, C, W, N, CH, NCH = (
        p.R, p.D, p.HC, p.FF, p.DF, p.F, p.C, p.W, p.N, p.CH, p.NCH
    )
    HF, Q, KR, H = R // 2, R // 4, (W + 1) * R, HC // HEAD_DIM
    RC = HF // NCHK
    base = p.base
    fs, z, t = lax.axis_index("fsdp"), lax.axis_index("ctx"), lax.axis_index("tp")
    core, yy, par = lax.rem(t, 2), t // 2, lax.rem(z, 2)
    to_core, to_y = {"tp": t + 1 - 2 * core}, {"tp": lax.rem(t + 2, 4)}
    to_next, to_prev = {"ctx": lax.rem(z + 1, C)}, {"ctx": lax.rem(z + C - 1, C)}
    to_pair = {"ctx": z + 1 - 2 * par}
    has_next, has_prev = z < C - 1, z > 0
    half = C // 2
    left_side = z < half
    hop = jnp.where(left_side, z, C - 1 - z)
    step_in = jnp.where(left_side, 1, -1)
    to_inner = {"ctx": z + step_in}
    to_outer = {"ctx": lax.rem(z - step_in + C, C)}
    is_outer, is_mid = hop == 0, hop == half - 1

    def owner(d):
        return lax.rem(fs + d, F)

    def rcopy(src, dst, k, dev):
        return pltpu.make_async_remote_copy(
            src_ref=src, dst_ref=dst, send_sem=ss.at[k], recv_sem=rs.at[k],
            device_id=dev, device_id_type=MESH,
        )

    unsent = []

    def send(src, dst, k, dev, cond=None):
        if cond is None:
            rcopy(src, dst, k, dev).start()
        else:
            pl.when(cond)(lambda: rcopy(src, dst, k, dev).start())
        unsent.append((src, k, cond))

    def got(dst, k):
        rcopy(dst, dst, k, to_core).wait_recv()

    def hint(i, m):
        return pl.multiple_of(i, m)

    def rows(off, n, m=16):
        return pl.ds(hint(off, m), n)

    local = []

    def fetch(src, dst):
        cp = pltpu.make_async_copy(src, dst, ls.at[len(local)])
        cp.start()
        local.append(cp)
        return cp

    own_half = rows(core * HF, HF)
    x_copy = fetch(v.x, v.XB.at[pl.ds(0, R)])
    own_cols = pl.ds(hint(fs * DF, 128), DF)

    def by_row(dst, col0, cols):
        def region(who, off, n):
            return dst.at[rows(who * DF + off, n), pl.ds(col0, cols)]
        return region

    def by_col(dst):
        def region(who, off, n):
            return dst.at[rows(off, n), pl.ds(hint(who * DF, 128), DF)]
        return region

    weights = (
        (v.wq, by_row(v.WQKV, 0, HC), 1), (v.wk, by_row(v.WQKV, HC, HC), 1),
        (v.wv, by_row(v.WQKV, 2 * HC, HC), 1), (v.wo, by_col(v.WO), 1),
        (v.wg, by_row(v.WG, 0, FF), 2), (v.wu, by_row(v.WU, 0, FF), 2), (v.wd, by_col(v.WD), 2),
    )
    gathers = []
    count = 0
    for source, region, parts in weights:
        tall = source.shape[0]
        cut = tall // 2 // parts
        gathers.append((
            source, fetch(source, region(fs, 0, tall)),
            [(region, tall // 2, k * cut, cut, count + k) for k in range(parts)],
        ))
        count += parts
    wq, wk, wv, wo, wg, wu, wd = gathers
    te_copy = fetch(v.teacher.at[own_half], v.TE)
    up_copy = fetch(v.upstream.at[own_half], v.UP)

    barrier = pltpu.get_barrier_semaphore()

    def greet(dev):
        pl.semaphore_signal(barrier, inc=1, device_id=dev, device_id_type=MESH)

    greet(to_core)
    greet(to_y)
    for d in range(1, F):
        greet({"fsdp": owner(d)})
    pl.when(has_next)(lambda: greet(to_next))
    pl.when(has_prev)(lambda: greet(to_prev))
    pl.semaphore_wait(
        barrier, 2 + F - 1 + has_next.astype(jnp.int32) + has_prev.astype(jnp.int32)
    )

    def piece_index(kind, number, d):
        return kind + number * (F - 1) + d - 1

    for source, _, pieces in gathers:
        for region, tall, at, n, number in pieces:
            for d in range(1, F):
                off = par * tall + at
                send(
                    source.at[rows(off, n)], region(fs, off, n), piece_index(base.wd, number, d),
                    {"fsdp": owner(d)},
                )

    def relay(weight, which):
        region, tall, at, n, number = weight[2][which]
        for d in range(1, F):
            part = region(owner(F - d), par * tall + at, n)
            got(part, piece_index(base.wd, number, d))
            send(part, part, piece_index(base.wr, number, d), to_pair)

    def relayed(weight):
        weight[1].wait()
        for region, tall, at, n, number in weight[2]:
            for d in range(1, F):
                got(region(owner(F - d), (1 - par) * tall + at, n), piece_index(base.wr, number, d))

    def x_half(j, which):
        return v.XB.at[rows(j * R + which * HF, HF)]

    send(v.x.at[own_half], x_half(1, core), base.xz, to_next, has_next)
    v.SG[0] = v.segment[...]
    send(v.segment, v.SG.at[1], base.sg, to_next, has_next)
    for j in range(1, W + 1):
        @pl.when(z < j)
        def _(j=j):
            v.XB[pl.ds(j * R, R), :] = jnp.zeros((R, D), bf16)
            v.SG[j] = jnp.full((1, R), -1, jnp.int32)

    def x_pass(j):
        @pl.when(z >= j)
        def _():
            got(x_half(j, core), base.xz + j - 1)
            got(v.SG.at[j], base.sg + j - 1)
        send(x_half(j, core), x_half(j, core), base.xc + j - 1, to_core, z >= j)
        if j < W:
            both = (z >= j) & has_next
            send(x_half(j, core), x_half(j + 1, core), base.xz + j, to_next, both)
            send(v.SG.at[j], v.SG.at[j + 1], base.sg + j, to_next, both)

    def x_done(j):
        pl.when(z >= j)(lambda: got(x_half(j, 1 - core), base.xc + j - 1))

    def norm_rows(j):
        def body(i, _):
            at = rows(j * R + i * RC, RC)
            xs = v.XB[at, :].astype(f32)
            r = lax.rsqrt(jnp.mean(xs * xs, axis=-1, keepdims=True) + EPS)
            v.N1[at, :] = (xs * r * v.gain_one[...]).astype(bf16)
            return 0
        lax.fori_loop(0, R // RC, body, 0)

    x_copy.wait()
    norm_rows(0)
    relay(wq, 0)
    relay(wk, 0)
    x_pass(1)
    relay(wv, 0)

    eye = lax.broadcasted_iota(jnp.int32, (R, R), 0) == lax.broadcasted_iota(jnp.int32, (R, R), 1)

    def column(row):
        return jnp.sum(jnp.where(eye, row.astype(f32), 0.0), axis=1, keepdims=True)

    v.VC[...] = jnp.broadcast_to(column(v.valid[...]), (R, 128))
    x_done(1)
    norm_rows(1)
    for j in range(2, W + 1):
        x_pass(j)
        x_done(j)
        norm_rows(j)
    seg_col = column(v.SG[0])
    for j in range(W + 1):
        same = seg_col == v.SG[j].astype(f32)
        if j == 0:
            same = same & (
                lax.broadcasted_iota(jnp.int32, (R, R), 1) <= lax.broadcasted_iota(jnp.int32, (R, R), 0)
            )
        v.BIAS[:, pl.ds(j * R, R)] = jnp.where(same, 0.0, -1e30)
    relayed(wq)
    v.QB[...] = jnp.dot(
        v.N1[pl.ds(0, R), :], v.WQKV[:, pl.ds(0, HC)], preferred_element_type=f32
    ).astype(bf16)
    relayed(wk)
    relayed(wv)
    for dst, col in ((v.KB, HC), (v.VB, 2 * HC)):
        dst[...] = jnp.dot(
            v.N1[...], v.WQKV[:, pl.ds(col, HC)], preferred_element_type=f32
        ).astype(bf16)
    relay(wo, 0)

    AR = 64 if R % 64 == 0 else R // 4

    def of_head(ref, h):
        val = ref[...]
        lane = lax.broadcasted_iota(jnp.int32, val.shape, 1) // HEAD_DIM
        return jnp.where(lane == h, val, jnp.zeros_like(val))

    def head_forward(h):
        v.S[...] = contract(of_head(v.QB, h), v.KB[...], (1, 1))

        def soft(i, _):
            at = rows(i * AR, AR)
            s = v.S[at, :] * (HEAD_DIM**-0.5) + v.BIAS[at, :]
            e = jnp.exp(s - jnp.max(s, axis=-1, keepdims=True))
            prob = e / jnp.sum(e, axis=-1, keepdims=True)
            v.PM[h, at, :] = prob
            v.PB[at, :] = prob.astype(bf16)
            return 0

        lax.fori_loop(0, R // AR, soft, 0)
        mix = jnp.dot(v.PB[...], of_head(v.VB, h), preferred_element_type=f32)
        v.O32[...] = v.O32[...] + mix

    v.O32[...] = jnp.zeros((R, HC), f32)
    lax.fori_loop(0, H, lambda h, _: (head_forward(h), 0)[1], 0)
    v.OB[...] = v.O32[...].astype(bf16)
    relay(wg, 0)

    def chunk(i):
        return pl.ds(i * RC, RC)

    def sum_begin(a, product):
        s1, r1, s2, r2 = v.S1.at[a], v.R1.at[a], v.S2.at[a], v.R2.at[a]
        s1[...] = product((1 - core) * HF).astype(bf16)
        for i in range(NCHK):
            send(s1.at[chunk(i)], r1.at[chunk(i)], base.a + a * NCHK + i, to_core)
        v.P32[...] = product(core * HF)
        for i in range(NCHK):
            got(r1.at[chunk(i)], base.a + a * NCHK + i)
            s2[chunk(i), :] = (v.P32[chunk(i), :] + r1[chunk(i), :].astype(f32)).astype(bf16)
            send(s2.at[chunk(i)], r2.at[chunk(i)], base.b + a * NCHK + i, to_y)

    def sum_end(a, i):
        s2, r2 = v.S2.at[a], v.R2.at[a]
        got(r2.at[chunk(i)], base.b + a * NCHK + i)
        return s2[chunk(i), :].astype(f32) + r2[chunk(i), :].astype(f32)

    def my_rows(i):
        return rows(core * HF + i * RC, RC)

    def their_rows(i):
        return rows((1 - core) * HF + i * RC, RC)

    def share(ref, flow, i):
        send(ref.at[my_rows(i)], ref.at[my_rows(i)], flow + i, to_core)

    def shared(ref, flow):
        for i in range(NCHK):
            got(ref.at[their_rows(i)], flow + i)

    relayed(wo)
    sum_begin(
        0,
        lambda off: jnp.dot(v.OB[rows(off, HF), :], v.WO[...], preferred_element_type=f32),
    )
    relay(wg, 1)
    for i in range(NCHK):
        h_now = v.XB[my_rows(i), :].astype(f32) + sum_end(0, i)
        v.H[chunk(i), :] = h_now
        r = lax.rsqrt(jnp.mean(h_now * h_now, axis=-1, keepdims=True) + EPS)
        v.N2[my_rows(i), :] = (h_now * r * v.gain_two[...]).astype(bf16)
        share(v.N2, base.n2, i)
    relay(wu, 0)
    relay(wu, 1)
    shared(v.N2, base.n2)

    relayed(wg)
    v.GB[...] = jnp.dot(v.N2[...], v.WG[...], preferred_element_type=f32).astype(bf16)
    relay(wd, 0)
    relayed(wu)
    v.UB[...] = jnp.dot(v.N2[...], v.WU[...], preferred_element_type=f32).astype(bf16)

    def activate(i, _):
        at = rows(i * RC, RC)
        g, u = v.GB[at, :].astype(f32), v.UB[at, :].astype(f32)
        v.AB[at, :] = (g / (1.0 + jnp.exp(-g)) * u).astype(bf16)
        return 0

    lax.fori_loop(0, R // RC, activate, 0)
    relay(wd, 1)
    relayed(wd)
    sum_begin(
        1,
        lambda off: jnp.dot(v.AB[rows(off, HF), :], v.WD[...], preferred_element_type=f32),
    )
    te_copy.wait()
    up_copy.wait()
    squares, counted = jnp.zeros((1, 1), f32), jnp.zeros((1, 1), f32)
    for i in range(NCHK):
        y_now = v.H[chunk(i), :] + sum_end(1, i)
        v.YB[my_rows(i), :] = y_now.astype(bf16)
        weighting = v.VC[my_rows(i), pl.ds(0, 1)]
        differ = y_now - v.TE[chunk(i), :].astype(f32)
        squares = squares + total_of(weighting * differ * differ)
        counted = counted + total_of(weighting)
        dy = v.UP[chunk(i), :].astype(f32) + weighting * differ
        v.DY[chunk(i), :] = dy
        v.DYB[my_rows(i), :] = dy.astype(bf16)
        share(v.DYB, base.dy, i)
    tile_row = lax.broadcasted_iota(jnp.int32, (8, 128), 0)
    v.LT[0] = jnp.where(
        tile_row == 0, jnp.broadcast_to(squares, (8, 128)), jnp.broadcast_to(counted, (8, 128))
    )
    send(v.LT.at[0], v.LT.at[1], base.lc, to_core)
    y_half = v.YB.at[own_half]
    send(y_half, y_half, base.yb, to_core)
    shared(v.DYB, base.dy)

    def weight_grad(left, right, at, d, tokens=R, col=None, n=None):
        who = owner(d)
        lhs = left[...] if col is None else left[pl.ds(0, tokens), pl.ds(col, n)]
        n = lhs.shape[1]
        if d == 0:
            own_done[0] = at + n
        rhs = right[pl.ds(0, tokens), pl.ds(hint(who * DF, 128), DF)]
        v.XS[who, pl.ds(at, n), :] = contract(lhs, rhs, (0, 0)).astype(bf16)

    def grad_index(d, j):
        return base.gx + (d - 1) * (NCH + 1) + j

    def grad_send(d, at, j):
        rcopy(
            v.XS.at[owner(d), at], v.XR.at[d - 1, at], grad_index(d, j), {"fsdp": owner(d)}
        ).start()

    sent, own_done = [0], [0]

    def grads_ready(upto):
        first, last = sent[0], upto // CH
        sent[0] = last

        def body(j, _):
            for d in range(1, F):
                grad_send(d, rows(j * CH, CH), j)
            return 0

        if last > first:
            lax.fori_loop(first, last, body, 0)

    def inward(at, j):
        for d in range(1, F):
            got(v.XR.at[d - 1, at], grad_index(d, j))
        acc = v.XS[fs, at, :].astype(f32)
        for d in range(1, F):
            acc = acc + v.XR[d - 1, at, :].astype(f32)
        v.SI[at, :] = acc.astype(bf16)

        @pl.when(jnp.logical_not(is_outer))
        def _():
            got(v.ZO.at[at], base.zin + j)
            v.SI[at, :] = (acc + v.ZO[at, :].astype(f32)).astype(bf16)

        @pl.when(is_mid)
        def _():
            rcopy(v.SI.at[at], v.ZI.at[at], base.zmid + j, to_inner).start()

        @pl.when(jnp.logical_not(is_mid))
        def _():
            rcopy(v.SI.at[at], v.ZO.at[at], base.zin + j, to_inner).start()

    def outward(at, j):
        @pl.when(is_mid)
        def _():
            got(v.ZI.at[at], base.zmid + j)
            whole = v.SI[at, :].astype(f32) + v.ZI[at, :].astype(f32)
            v.GRAD[at, :] = whole.astype(bf16)

        @pl.when(jnp.logical_not(is_mid))
        def _():
            got(v.ZI.at[at], base.zout + j)
            v.GRAD[at, :] = v.ZI[at, :]

        @pl.when(jnp.logical_not(is_outer))
        def _():
            rcopy(v.GRAD.at[at], v.ZI.at[at], base.zout + j, to_outer).start()

    lag_in, lag_out = SKEW * hop, SKEW * (2 * half - 1 - hop)
    LAST = NCH + SKEW * (2 * half - 1)

    def pump(first, last):
        def body(i, _):
            ja, jb = i - lag_in, i - lag_out
            pl.when((ja >= 0) & (ja < NCH))(lambda: inward(rows(ja * CH, CH), ja))
            pl.when((jb >= 0) & (jb < NCH))(lambda: outward(rows(jb * CH, CH), jb))
            return 0

        if last > first:
            lax.fori_loop(first, last, body, 0)

    pumped = [0]

    def pump_to(last):
        ready = min(sent[0], own_done[0] // CH)
        last = min(last, ready if ready < NCH else LAST)
        if last > pumped[0]:
            pump(pumped[0], last)
            pumped[0] = last

    peers = range(1, F)
    for d in peers:
        weight_grad(v.AB, v.DYB, 0, d)
    grads_ready(FF)
    v.DA32[...] = contract(v.DYB[...], v.WD[...], (1, 1))

    def activate_back(i, _):
        at = rows(i * RC, RC)
        g, u, da = v.GB[at, :].astype(f32), v.UB[at, :].astype(f32), v.DA32[at, :]
        sig = 1.0 / (1.0 + jnp.exp(-g))
        v.DGB[at, :] = (da * u * (sig * (1.0 + g * (1.0 - sig)))).astype(bf16)
        v.DUB[at, :] = (da * (g * sig)).astype(bf16)
        return 0

    lax.fori_loop(0, R // RC, activate_back, 0)
    sum_begin(
        2,
        lambda off: contract(v.DGB[rows(off, HF), :], v.WG[...], (1, 1))
        + contract(v.DUB[rows(off, HF), :], v.WU[...], (1, 1)),
    )
    weight_grad(v.AB, v.DYB, 0, 0)
    for d in peers:
        weight_grad(v.DGB, v.N2, FF, d)
    grads_ready(2 * FF)
    pump_to(2)
    for i in range(NCHK):
        dn2 = sum_end(2, i)
        h_now = v.H[chunk(i), :]
        r = lax.rsqrt(jnp.mean(h_now * h_now, axis=-1, keepdims=True) + EPS)
        gd = v.gain_two[...] * dn2
        dh = v.DY[chunk(i), :] + r * gd - h_now * (
            r * r * r * jnp.mean(gd * h_now, axis=-1, keepdims=True)
        )
        v.DH[chunk(i), :] = dh
        v.DHB[my_rows(i), :] = dh.astype(bf16)
        share(v.DHB, base.dh, i)
        part = jnp.sum(dn2 * h_now * r, axis=0, keepdims=True)
        part = jnp.where(yy == i // (NCHK // 2), part, 0.0)
        if i == 0:
            v.GT[0] = jnp.zeros((8, D), f32)
        v.GT[0, pl.ds(0, 1), :] = v.GT[0, pl.ds(0, 1), :] + part
    for d in peers:
        weight_grad(v.DUB, v.N2, 2 * FF, d)
    grads_ready(3 * FF)
    weight_grad(v.DGB, v.N2, FF, 0)
    weight_grad(v.DUB, v.N2, 2 * FF, 0)
    shared(v.DHB, base.dh)
    v.DOB[...] = contract(v.DHB[...], v.WO[...], (1, 1)).astype(bf16)
    pump_to(6)
    for d in peers:
        weight_grad(v.OB, v.DHB, 3 * FF, d)
    grads_ready(3 * FF + HC)
    weight_grad(v.OB, v.DHB, 3 * FF, 0)
    pump_to(10)

    v.O32[...] = jnp.zeros((R, HC), f32)
    v.DK32[...] = jnp.zeros((KR, HC), f32)
    v.DV32[...] = jnp.zeros((KR, HC), f32)

    def head_backward(h):
        doh = of_head(v.DOB, h)
        v.S[...] = contract(doh, v.VB[...], (1, 1))

        def soft_back(i, _):
            at = rows(i * AR, AR)
            prob, dp = v.PM[h, at, :], v.S[at, :]
            ds = prob * (dp - jnp.sum(prob * dp, axis=-1, keepdims=True))
            v.PB[at, :] = prob.astype(bf16)
            v.DSB[at, :] = ds.astype(bf16)
            return 0

        lax.fori_loop(0, R // AR, soft_back, 0)
        v.DV32[...] = v.DV32[...] + contract(v.PB[...], doh, (0, 0))
        v.O32[...] = v.O32[...] + jnp.dot(
            v.DSB[...], of_head(v.KB, h), preferred_element_type=f32
        )
        v.DK32[...] = v.DK32[...] + contract(v.DSB[...], of_head(v.QB, h), (0, 0))

    lax.fori_loop(0, H, lambda h, _: (head_backward(h), 0)[1], 0)
    scale = HEAD_DIM**-0.5
    v.DALL[pl.ds(0, R), pl.ds(0, HC)] = (v.O32[...] * scale).astype(bf16)
    v.DALL[:, pl.ds(HC, HC)] = (v.DK32[...] * scale).astype(bf16)
    v.DALL[:, pl.ds(2 * HC, HC)] = v.DV32[...].astype(bf16)
    pump_to(16)

    def dn1_product(j, which):
        at = rows(j * R + which * HF, HF)
        c0 = 0 if j == 0 else HC
        return contract(
            v.DALL[at, pl.ds(c0, 3 * HC - c0)], v.WQKV[:, pl.ds(c0, 3 * HC - c0)], (1, 1)
        )

    for j in range(W, -1, -1):
        v.D1S[j] = dn1_product(j, 1 - core).astype(bf16)
        send(v.D1S.at[j], v.D1R.at[j], base.d1 + j, to_core)
        v.D1O[j] = dn1_product(j, core)
    for d in list(peers) + [0]:
        at = 3 * FF + HC
        weight_grad(v.DALL, v.N1, at, d, R, 0, HC)
        weight_grad(v.DALL, v.N1, at + HC, d, KR, HC, HC)
        weight_grad(v.DALL, v.N1, at + 2 * HC, d, KR, 2 * HC, HC)
        if d == F - 1:
            grads_ready(N)
    for j in range(W, -1, -1):
        got(v.D1R.at[j], base.d1 + j)
        there = rows((1 - yy) * Q, Q)
        v.D2S[j] = (v.D1O[j, there, :] + v.D1R[j, there, :].astype(f32)).astype(bf16)
        send(v.D2S.at[j], v.D2R.at[j], base.d2 + j, to_y)
    pump_to(20)
    here = rows(yy * Q, Q)
    for j in range(W, 0, -1):
        got(v.D2R.at[j], base.d2 + j)
        own = v.D1O[j, here, :] + v.D1R[j, here, :].astype(f32) + v.D2R[j].astype(f32)
        v.DZS[j] = own.astype(bf16)
        if j < W:
            @pl.when(has_next & (z >= j))
            def _(j=j, own=own):
                got(v.DZR.at[j + 1], base.dz + j + 1)
                v.DZS[j] = (own + v.DZR[j + 1].astype(f32)).astype(bf16)
        send(v.DZS.at[j], v.DZR.at[j], base.dz + j, to_prev, z >= j)
        pump_to(26 + 3 * (W - j))

    got(v.LT.at[1], base.lc)
    v.LB[z] = v.LT[0] + v.LT[1]
    for s in range(C - 1):
        left_tile, right_tile = z - s, z + s
        send(v.LB.at[jnp.maximum(left_tile, 0)], v.LB.at[jnp.maximum(left_tile, 0)],
             base.lr + s, to_next, has_next & (left_tile >= 0))
        send(v.LB.at[jnp.minimum(right_tile, C - 1)], v.LB.at[jnp.minimum(right_tile, C - 1)],
             base.ll + s, to_prev, has_prev & (right_tile <= C - 1))
        if s == 0:
            pump_to(30)
        pl.when(left_tile - 1 >= 0)(
            lambda i=left_tile - 1, s=s: got(v.LB.at[jnp.maximum(i, 0)], base.lr + s)
        )
        pl.when(right_tile + 1 <= C - 1)(
            lambda i=right_tile + 1, s=s: got(v.LB.at[jnp.minimum(i, C - 1)], base.ll + s)
        )
    v.LX[fs] = v.LB[...]
    for d in peers:
        send(v.LB, v.LX.at[fs], base.lx + d - 1, {"fsdp": owner(d)})

    pump_to(34)
    got(v.D2R.at[0], base.d2)
    v.P32[pl.ds(0, Q), :] = (
        v.D1O[0, here, :] + v.D1R[0, here, :].astype(f32) + v.D2R[0].astype(f32)
    )

    @pl.when(has_next)
    def _():
        got(v.DZR.at[1], base.dz + 1)
        v.P32[pl.ds(0, Q), :] = v.P32[pl.ds(0, Q), :] + v.DZR[1].astype(f32)

    quarter = rows(core * HF + yy * Q, Q)
    dn1 = v.P32[pl.ds(0, Q), :]
    x_now = v.XB[quarter, :].astype(f32)
    r = lax.rsqrt(jnp.mean(x_now * x_now, axis=-1, keepdims=True) + EPS)
    gd = v.gain_one[...] * dn1
    gi = v.DH[here, :] + r * gd - x_now * (
        r * r * r * jnp.mean(gd * x_now, axis=-1, keepdims=True)
    )
    v.GIB[quarter, :] = gi.astype(bf16)
    mine = v.GIB.at[quarter]
    send(mine, mine, base.i1, to_y)
    send(mine, mine, base.i2, to_core)
    v.GT[0, pl.ds(1, 1), :] = jnp.sum(dn1 * x_now * r, axis=0, keepdims=True)
    send(v.GT.at[0], v.GR.at[0], base.g1, to_core)
    pump_to(38)
    got(v.GR.at[0], base.g1)
    v.GT[1] = v.GT[0] + v.GR[0]
    send(v.GT.at[1], v.GR.at[1], base.g2, to_y)
    from_y = v.GIB.at[rows(core * HF + (1 - yy) * Q, Q)]
    got(from_y, base.i1)
    send(from_y, from_y, base.i3, to_core)
    pump_to(42)
    got(v.GR.at[1], base.g2)
    v.GT[2] = v.GT[1] + v.GR[1]
    for d in list(peers) + [0]:
        tile = v.GT[2, :, pl.ds(hint(owner(d) * DF, 128), DF)]
        v.XS[owner(d), pl.ds(N, 16), :] = jnp.concatenate([tile, jnp.zeros_like(tile)], 0).astype(bf16)
        if d:
            grad_send(d, pl.ds(N, 16), NCH)

    for d in peers:
        got(v.LX.at[owner(F - d)], base.lx + d - 1)
    sums = [sum(v.LX[s, c] for c in range(C)) for s in range(F)]
    counted = sum(s[1:2, :] for s in sums)
    for s in range(F):
        v.LOSS[pl.ds(s, 1), :] = sums[s][0:1, :] * F / (counted * D)

    pump_to(LAST - SKEW * (2 * half - 1))
    gain_rows = pl.ds(N, 16)
    inward(gain_rows, NCH)
    pump_to(LAST)
    outward(gain_rows, NCH)
    got(v.YB.at[rows((1 - core) * HF, HF)], base.yb)
    got(v.GIB.at[rows((1 - core) * HF + yy * Q, Q)], base.i2)
    got(v.GIB.at[rows((1 - core) * HF + (1 - yy) * Q, Q)], base.i3)

    def left(src, k):
        rcopy(src, src, k, to_core).wait_send()

    for src, k, cond in unsent:
        if cond is None:
            left(src, k)
        else:
            pl.when(cond)(functools.partial(left, src, k))

    def drain(at, j):
        for d in peers:
            left(v.XS.at[owner(d), at], grad_index(d, j))
        pl.when(is_mid)(lambda: left(v.SI.at[at], base.zmid + j))
        pl.when(jnp.logical_not(is_mid))(lambda: left(v.SI.at[at], base.zin + j))
        pl.when(jnp.logical_not(is_outer))(lambda: left(v.GRAD.at[at], base.zout + j))

    lax.fori_loop(0, NCH, lambda j, _: (drain(rows(j * CH, CH), j), 0)[1], 0)
    drain(gain_rows, NCH)


def finish_kernel(p, grad, gib, yb, loss, y_out, loss_out, gi_out, one, gq, gk, gv, go, two, gg, gu, gd):
    FF, HC, N = p.FF, p.HC, p.N
    y_out[0] = yb[...]
    gi_out[0] = gib[...].astype(f32)
    at = 3 * FF
    gd[...] = grad[pl.ds(0, FF), :].astype(f32)
    go[...] = grad[pl.ds(at, HC), :].astype(f32)
    for ref, first, n in (
        (gg, FF, FF), (gu, 2 * FF, FF), (gq, at + HC, HC), (gk, at + 2 * HC, HC), (gv, at + 3 * HC, HC),
    ):
        for c in range(0, n, 128):
            w = min(128, n - c)
            ref[:, pl.ds(c, w)] = grad[pl.ds(first + c, w), :].astype(f32).T
    gains = grad[pl.ds(N, 16), :].astype(f32)
    two[...] = gains[0:1, :]
    one[...] = gains[1:2, :]
    for s in range(p.F):
        loss_out[s] = jnp.max(loss[pl.ds(s, 1), :])


def shards(mesh_shape, seq_len, *args):
    (inputs, upstream, teacher, valid, segment, gain_one, wq, wk, wv, wo, gain_two, wg, wu, wd) = args
    _, rows_here, width = inputs.shape
    p = Plan(
        mesh_shape["fsdp"], mesh_shape["ctx"], rows_here, width, wq.shape[1], wg.shape[1], seq_len
    )
    R, D, DF, HC, FF, F = p.R, p.D, p.DF, p.HC, p.FF, p.F
    NG = p.N + 16
    scratch = scratch_of(p)
    vmem = pl.BlockSpec(memory_space=pltpu.VMEM)
    anywhere = pl.BlockSpec(memory_space=pl.ANY)
    in_specs = [anywhere] * 3 + [vmem] * 3 + [anywhere] * 4 + [vmem] + [anywhere] * 3
    sds = jax.ShapeDtypeStruct
    grad, gib, yb, loss = pl.pallas_call(
        functools.partial(layer_kernel, p, tuple(scratch)),
        out_shape=(
            sds((NG, DF), bf16), sds((R, D), bf16), sds((R, D), bf16), sds((max(F, 8), 128), f32),
        ),
        in_specs=in_specs,
        out_specs=(vmem,) * 4,
        scratch_shapes=[pltpu.VMEM(s, dt) for s, dt in scratch.values()]
        + [
            pltpu.SemaphoreType.DMA((p.total,)), pltpu.SemaphoreType.DMA((p.total,)),
            pltpu.SemaphoreType.DMA((10,)),
        ],
        compiler_params=pltpu.CompilerParams(
            collective_id=0, has_side_effects=True, vmem_limit_bytes=67043328
        ),
        name="layer",
    )(
        inputs.reshape(R, D), upstream.reshape(R, D), teacher.reshape(R, D), valid, segment,
        gain_one.reshape(1, D), wq, wk, wv, wo, gain_two.reshape(1, D), wg, wu, wd,
    )
    outs = pl.pallas_call(
        functools.partial(finish_kernel, p),
        out_shape=(
            sds((1, R, D), bf16), sds((F,), f32), sds((1, R, D), f32), sds((1, DF), f32),
            sds((DF, HC), f32), sds((DF, HC), f32), sds((DF, HC), f32), sds((HC, DF), f32),
            sds((1, DF), f32), sds((DF, FF), f32), sds((DF, FF), f32), sds((FF, DF), f32),
        ),
        in_specs=[vmem] * 4,
        out_specs=(vmem, pl.BlockSpec(memory_space=pltpu.SMEM)) + (vmem,) * 10,
        compiler_params=pltpu.CompilerParams(vmem_limit_bytes=40 * 2**20),
        name="finish",
    )(grad, gib, yb, loss)
    outs = list(outs)
    outs[3], outs[8] = outs[3].reshape(DF), outs[8].reshape(DF)
    return tuple(outs)


def solution(mesh):
    def run(*args):
        token, row, col = P("fsdp", "ctx", None), P("fsdp", "tp"), P("tp", "fsdp")
        pair = P("fsdp", "ctx")
        return jax.shard_map(
            functools.partial(shards, dict(mesh.shape), args[0].shape[1]),
            mesh=mesh,
            in_specs=(token, token, token, pair, pair, P(), row, row, row, col, P(), row, row, col),
            out_specs=(
                token, P(), token, P("fsdp"), row, row, row, col, P("fsdp"), row, row, col,
            ),
            check_vma=False,
        )(*args)

    return run
```

time: 630 us -> 201 us (0.32)
  waiting for transfers between devices: 443 us -> 0 us
  Pallas kernels: 0 us -> 189 us
  blocking collectives: 83.5 us -> 0 us
  matrix products: 42 us -> 0 us
  other arithmetic: 36.8 us -> 0 us
  between operations: 17.6 us -> 0.68 us
    psum x5 -> x0, waiting for transfers between devices: 224 us -> none  [the longest x4 120 us: head_total(): return lax.psum(partial_sum, 'tp')]
    pallas_call x0 -> x2, Pallas kernels: none -> 189 us  [the longest x1 186 us: shards(): pl.pallas_call(functools.partial(layer_kernel, p, tuple(scratch)), out_sh...]
    reduce_scatter x8 -> x0, waiting for transfers between devices: 176 us -> none  [the longest x1 30.8 us: shards(): lax.psum_scatter(pair_terms, 'ctx', scatter_dimension=1, tiled=True)]
    all_gather x5 -> x0, blocking collectives: 45.1 us -> none  [the longest x1 11.1 us: shards(): seg_whole = lax.all_gather(segment, 'ctx', axis=1, tiled=True)]
    dot_general x27 -> x0, matrix products: 42 us -> none  [the longest x20 28.2 us: contract(): return jnp.einsum(pattern, left, right, preferred_element_type=jnp.float32)]
    all_gather x4 -> x0, waiting for transfers between devices: 41.3 us -> none  [the longest x1 24 us: shards(): lax.all_gather(down_weight, 'fsdp', axis=1, tiled=True)]
    psum x2 -> x0, blocking collectives: 33.5 us -> none  [the longest x1 21.2 us: shards(): counted, squared = lax.psum((jnp.sum(weighting), placed), ('fsdp', 'ctx'))]
    convert_element_type x12 -> x0, other arithmetic: 15 us -> none  [the longest x1 2.41 us: shards(): lax.psum(row_gate.astype(jnp.bfloat16), 'ctx').astype(jnp.float32)]
  transfers between devices with their start and end apart: 17 -> 0, of which waited for: 16 -> 0; matrix products, arithmetic and copies ran while one was open for 6% -> 0% of each run, Pallas kernels for 0% -> 0%
where the time goes in v1:
time: 201 us
  Pallas kernels  189 us (94%)
  local copies, waits for them, and re-layouts  11.3 us (6%)
    pallas_call x1, Pallas kernels, shards(): pl.pallas_call(functools.partial(layer_kernel, p, tuple(scratch)), out_sh...  186 us
    unnamed x14, local copies, waits for them, and re-layouts  11.3 us

profile of v1, /device:TPU:0, one launch (start us, length us, event | category | flops | bytes accessed | tf_op | source)
XLA Modules:
  0.0 201.0 jit_solution(17016291644542665271)
XLA Ops:
  0.6 0.0 copy-start.4
  0.7 2.3 %copy.26.refs_11_ = bf16[512,704]{1,0:T(8,128)(2,1)} copy(bf16[512,704]{0,1:T(8,128)(2,1)} %param.25) | data formatting | bytes 1441792 | tf_op args[11]
  3.0 0.0 copy-done.4
  3.0 1.2 copy.27.refs_12_
  4.1 186.2 %layer.1 = (bf16[3152,512]{1,0:T(8,128)(2,1)}, bf16[256,1024]{1,0:T(8,128)(2,1)}, bf16[256,1024]{1,0:T(8,128)(2,1)}, f32[8,128]{1,0:T(8,128)}) custom-call(bf16[256,1024]{1,0:T(8,128)(2,1)} %bitcast.7, bf16[256,1024]{1,0:T(8,128)(2,1)} %bitcast.8, bf16[256,1024]{1,0:T(8,128)(2,1)} %bitcast.9, s32[1,256]{1,0:T(1,128)} %refs_3_.1, s32[1,256]{1,0:T(1,128)} %refs_4_.1, ...), custom_call_target="tpu_custom_call" | custom-call | tf_op jit(solution)/shard_map/layer/pallas_call | solution.py:749
  190.3 0.0 copy-start
  190.3 1.9 copy-done
  192.2 0.0 copy-start.1
  192.2 1.0 copy-done.1
  193.3 0.0 copy-start.2
  193.3 1.0 copy-done.2
  194.3 0.0 copy-start.3
  194.3 0.7 copy-done.3
  195.0 2.9 %finish.1 = (bf16[1,256,1024]{2,1,0:T(8,128)(2,1)}, f32[2]{0:T(128)}, f32[1,256,1024]{2,1,0:T(8,128)}, f32[1,512]{1,0:T(1,128)}, f32[512,256]{1,0:T(8,128)}, /*i...) custom-call(bf16[3152,512]{1,0:T(8,128)(2,1)S(1)} %copy-done, ...), custom_call_target="tpu_custom_call" | custom-call | tf_op jit(solution)/shard_map/finish/pallas_call | solution.py:769
  197.9 1.6 copy.28
  199.5 1.6 copy.29
Async XLA Ops:
  0.6 2.3 %copy-start.4 = (bf16[512,704]{0,1:T(8,128)(2,1)S(1)}, bf16[512,704]{0,1:T(8,128)(2,1)}, u32[]{:S(2)}) copy-start(bf16[512,704]{0,1:T(8,128)(2,1)} %param.26) | copy-start | bytes 2162692
  190.3 1.9 copy-start
  192.2 1.0 copy-start.1
  193.3 1.0 copy-start.2
  194.3 0.7 copy-start.3

commit v2 on v1

v2 whole, which is shorter than its diff:
```python
import functools
from types import SimpleNamespace

import jax
import jax.numpy as jnp
from jax import lax
from jax.experimental import pallas as pl
from jax.experimental.pallas import tpu as pltpu
from jax.sharding import PartitionSpec as P

HEAD_DIM = 64
EPS = 1e-05
MESH = pl.DeviceIdType.MESH
NCHK = 4
SKEW = 3
f32, bf16 = jnp.float32, jnp.bfloat16


class Plan:
    def __init__(self, fsdp, ctx, rows, width, head_cols, hidden, seq_len):
        self.F, self.C, self.R, self.D = fsdp, ctx, rows, width
        self.HC, self.FF = head_cols, hidden
        self.DF = width // fsdp
        self.W = -(-(seq_len // 2) // rows)
        self.N = 3 * hidden + 4 * head_cols
        self.CH = next(
            k for k in range(16, self.N + 1, 16) if self.N % k == 0 and k * self.DF >= 32768
        )
        self.NCH = self.N // self.CH
        self.base, self.total = SimpleNamespace(), 0
        peers = fsdp - 1
        for name, count in dict(
            xz=self.W, sg=self.W, xy=self.W, xc=self.W, wd=10 * peers, wr=10 * peers,
            a=3 * NCHK, b=3 * NCHK, n2=NCHK, yb=1, dy=NCHK, dh=NCHK,
            lc=1, lr=ctx, ll=ctx, lx=peers, d1=self.W + 1, d2=self.W + 1, dz=self.W + 1,
            g1=1, g2=1, i1=1, i2=1, i3=1, gx=peers * (self.NCH + 1),
            zo=self.NCH + 1, zi=self.NCH + 1,
        ).items():
            setattr(self.base, name, self.total)
            self.total += count
        self.sends = 4 * self.W + 2 + 14 * peers + 9 + 3 + 2 * ctx + peers + 3 * self.W + 2 + 5 + peers + 2


def contract(left, right, dims):
    return lax.dot_general(left, right, ((dims[:1], dims[1:]), ((), ())), preferred_element_type=f32)


def total_of(v):
    return jnp.sum(jnp.sum(v, axis=1, keepdims=True), axis=0, keepdims=True)


def scratch_of(p):
    R, D, HC, FF, DF, F, C, W = p.R, p.D, p.HC, p.FF, p.DF, p.F, p.C, p.W
    HF, Q, KR, H = R // 2, R // 4, (p.W + 1) * p.R, p.HC // HEAD_DIM
    NG = p.N + 16
    return dict(
        XB=((KR, D), bf16), SG=((W + 1, 1, R), jnp.int32), N1=((KR, D), bf16),
        WQKV=((D, 3 * HC), bf16), WO=((HC, D), bf16), WG=((FF, D), bf16),
        WU=((FF, D), bf16), WD=((FF, D), bf16),
        QH=((H * R, HC), bf16), KB=((KR, HC), bf16), VB=((KR, HC), bf16), DOH=((H * R, HC), bf16),
        PM=((H * R, W * R), f32), S=((H * R, KR), f32), PB=((H * R, KR), bf16), DSB=((H * R, KR), bf16),
        BIAS=((R, W * R), f32), DQ=((R, HC), bf16), DKT=((HC, KR), bf16), DVT=((HC, KR), bf16),
        OB=((R, HC), bf16), VC=((R, 128), f32),
        H=((HF, D), f32), DY=((HF, D), f32), DH=((HF, D), f32), P32=((HF, D), f32),
        UP=((HF, D), bf16), TE=((HF, D), bf16),
        N2=((R, D), bf16), DYB=((R, D), bf16), DHB=((R, D), bf16),
        GB=((R, FF), bf16), UB=((R, FF), bf16), AB=((R, FF), bf16),
        DGB=((R, FF), bf16), DUB=((R, FF), bf16),
        D1S=((W + 1, HF, D), bf16), D1R=((W + 1, HF, D), bf16), D1O=((W + 1, HF, D), f32),
        D2S=((W + 1, Q, D), bf16), D2R=((W + 1, Q, D), bf16), DZR=((W + 1, Q, D), bf16),
        DZS=((W + 1, Q, D), bf16),
        GT=((3, 8, D), f32), GR=((2, 8, D), f32),
        LT=((2, 8, 128), f32), LB=((C, 8, 128), f32), LX=((F, C, 8, 128), f32),
        XS=((F, NG, DF), bf16), XR=((F - 1, NG, DF), bf16),
        ZO=((NG, DF), bf16), ZI=((NG, DF), bf16), GRAD=((NG, DF), bf16), GIB=((R, D), bf16),
        YB=((R, D), bf16), LOSS=((max(F, 8), 128), f32),
        S1=((3, HF, D), bf16), R1=((3, HF, D), bf16), S2=((3, HF, D), bf16), R2=((3, HF, D), bf16),
    )


def layer_kernel(p, names, *refs):
    v = SimpleNamespace(**dict(zip(names, refs[18:], strict=False)))
    (
        v.x, v.upstream, v.teacher, v.valid, v.segment, v.gain_one, v.wq, v.wk, v.wv, v.wo,
        v.gain_two, v.wg, v.wu, v.wd, v.grad_out, v.gi_out, v.y_out, v.loss_out,
    ) = refs[:18]
    ss, rs, ls = refs[-3:]
    R, D, HC, FF, DF, F, C, W, N, CH, NCH = (
        p.R, p.D, p.HC, p.FF, p.DF, p.F, p.C, p.W, p.N, p.CH, p.NCH
    )
    HF, Q, KR, H = R // 2, R // 4, (W + 1) * R, HC // HEAD_DIM
    RC = HF // NCHK
    base = p.base
    fs, z, t = lax.axis_index("fsdp"), lax.axis_index("ctx"), lax.axis_index("tp")
    core, yy, par = lax.rem(t, 2), t // 2, lax.rem(z, 2)
    to_core, to_y = {"tp": t + 1 - 2 * core}, {"tp": lax.rem(t + 2, 4)}
    to_next, to_prev = {"ctx": lax.rem(z + 1, C)}, {"ctx": lax.rem(z + C - 1, C)}
    to_pair = {"ctx": z + 1 - 2 * par}
    has_next, has_prev = z < C - 1, z > 0
    half = C // 2
    left_side = z < half
    hop = jnp.where(left_side, z, C - 1 - z)
    step_in = jnp.where(left_side, 1, -1)
    to_inner = {"ctx": z + step_in}
    to_outer = {"ctx": lax.rem(z - step_in + C, C)}
    is_outer, is_mid = hop == 0, hop == half - 1

    def owner(d):
        return lax.rem(fs + d, F)

    def rcopy(src, dst, sk, rk, dev):
        return pltpu.make_async_remote_copy(
            src_ref=src, dst_ref=dst, send_sem=ss.at[sk], recv_sem=rs.at[rk],
            device_id=dev, device_id_type=MESH,
        )

    unsent = []

    def outgoing(src, cond=None):
        unsent.append((src, cond))
        assert len(unsent) <= p.sends
        return len(unsent) - 1

    def send(src, dst, k, dev, cond=None, group=None):
        sk = outgoing(src, cond) if group is None else group
        if cond is None:
            rcopy(src, dst, sk, k, dev).start()
        else:
            pl.when(cond)(lambda: rcopy(src, dst, sk, k, dev).start())

    def got(dst, k):
        rcopy(dst, dst, 0, k, to_core).wait_recv()

    def hint(i, m):
        return pl.multiple_of(i, m)

    def rows(off, n, m=16):
        return pl.ds(hint(off, m), n)

    local = []

    def fetch(src, dst):
        cp = pltpu.make_async_copy(src, dst, ls.at[len(local)])
        cp.start()
        local.append(cp)
        return cp

    own_half = rows(core * HF, HF)
    x_copy = fetch(v.x, v.XB.at[pl.ds(0, R)])
    own_cols = pl.ds(hint(fs * DF, 128), DF)

    def by_row(dst, col0, cols):
        def region(who, off, n):
            return dst.at[rows(who * DF + off, n), pl.ds(col0, cols)]
        return region

    def by_col(dst):
        def region(who, off, n):
            return dst.at[rows(off, n), pl.ds(hint(who * DF, 128), DF)]
        return region

    weights = (
        (v.wq, by_row(v.WQKV, 0, HC), 1), (v.wk, by_row(v.WQKV, HC, HC), 1),
        (v.wv, by_row(v.WQKV, 2 * HC, HC), 1), (v.wo, by_col(v.WO), 1),
        (v.wg, by_col(v.WG), 2), (v.wu, by_col(v.WU), 2), (v.wd, by_col(v.WD), 2),
    )
    gathers = []
    count = 0
    for source, region, parts in weights:
        tall = source.shape[0]
        cut = tall // 2 // parts
        gathers.append((
            source, fetch(source, region(fs, 0, tall)),
            [(region, tall // 2, k * cut, cut, count + k) for k in range(parts)],
        ))
        count += parts
    wq, wk, wv, wo, wg, wu, wd = gathers
    te_copy = fetch(v.teacher.at[own_half], v.TE)
    up_copy = fetch(v.upstream.at[own_half], v.UP)

    barrier = pltpu.get_barrier_semaphore()

    def greet(dev):
        pl.semaphore_signal(barrier, inc=1, device_id=dev, device_id_type=MESH)

    greet(to_core)
    greet(to_y)
    for d in range(1, F):
        greet({"fsdp": owner(d)})
    pl.when(has_next)(lambda: greet(to_next))
    pl.when(has_prev)(lambda: greet(to_prev))
    pl.semaphore_wait(
        barrier, 2 + F - 1 + has_next.astype(jnp.int32) + has_prev.astype(jnp.int32)
    )

    def piece_index(kind, number, d):
        return kind + number * (F - 1) + d - 1

    for source, _, pieces in gathers:
        tall = source.shape[0] // 2
        for d in range(1, F):
            group = outgoing(source.at[rows(par * tall, tall)])
            for region, _, at, n, number in pieces:
                off = par * tall + at
                send(
                    source.at[rows(off, n)], region(fs, off, n), piece_index(base.wd, number, d),
                    {"fsdp": owner(d)}, None, group,
                )

    relays = {}

    def relay(weight, which):
        region, tall, at, n, number = weight[2][which]
        for d in range(1, F):
            if which == 0:
                relays[number, d] = outgoing(region(owner(F - d), par * tall, tall))
            part = region(owner(F - d), par * tall + at, n)
            got(part, piece_index(base.wd, number, d))
            send(
                part, part, piece_index(base.wr, number, d), to_pair, None, relays[number - which, d]
            )

    def relayed(weight):
        weight[1].wait()
        for region, tall, at, n, number in weight[2]:
            for d in range(1, F):
                got(region(owner(F - d), (1 - par) * tall + at, n), piece_index(base.wr, number, d))

    def x_half(j, which):
        return v.XB.at[rows(j * R + which * HF, HF)]

    def x_quarter(j, y):
        return v.XB.at[rows(j * R + core * HF + y * Q, Q)]

    send(v.x.at[rows(core * HF + yy * Q, Q)], x_quarter(1, yy), base.xz, to_next, has_next)
    v.SG[0] = v.segment[...]
    send(v.segment, v.SG.at[1], base.sg, to_next, has_next)
    for j in range(1, W + 1):
        @pl.when(z < j)
        def _(j=j):
            v.XB[pl.ds(j * R, R), :] = jnp.zeros((R, D), bf16)
            v.SG[j] = jnp.full((1, R), -1, jnp.int32)

    def x_pass(j):
        @pl.when(z >= j)
        def _():
            got(x_quarter(j, yy), base.xz + j - 1)
            got(v.SG.at[j], base.sg + j - 1)
        if j < W:
            both = (z >= j) & has_next
            send(x_quarter(j, yy), x_quarter(j + 1, yy), base.xz + j, to_next, both)
            send(v.SG.at[j], v.SG.at[j + 1], base.sg + j, to_next, both)
        send(x_quarter(j, yy), x_quarter(j, yy), base.xy + j - 1, to_y, z >= j)

    def x_join(j):
        pl.when(z >= j)(lambda: got(x_quarter(j, 1 - yy), base.xy + j - 1))
        send(x_half(j, core), x_half(j, core), base.xc + j - 1, to_core, z >= j)

    def x_done(j):
        pl.when(z >= j)(lambda: got(x_half(j, 1 - core), base.xc + j - 1))

    def norm_rows(j):
        def body(i, _):
            at = rows(j * R + i * RC, RC)
            xs = v.XB[at, :].astype(f32)
            r = lax.rsqrt(jnp.mean(xs * xs, axis=-1, keepdims=True) + EPS)
            v.N1[at, :] = (xs * r * v.gain_one[...]).astype(bf16)
            return 0
        lax.fori_loop(0, R // RC, body, 0)

    eye = lax.broadcasted_iota(jnp.int32, (R, R), 0) == lax.broadcasted_iota(jnp.int32, (R, R), 1)
    lower = lax.broadcasted_iota(jnp.int32, (R, R), 1) <= lax.broadcasted_iota(jnp.int32, (R, R), 0)

    def column(row):
        return jnp.sum(jnp.where(eye, row.astype(f32), 0.0), axis=1, keepdims=True)

    x_copy.wait()
    norm_rows(0)
    v.VC[...] = jnp.broadcast_to(column(v.valid[...]), (R, 128))
    relay(wq, 0)
    x_pass(1)
    relay(wk, 0)
    relay(wv, 0)
    x_join(1)
    x_done(1)
    norm_rows(1)
    for j in range(2, W + 1):
        x_pass(j)
        if j == 2:
            relay(wo, 0)
            relay(wg, 0)
        x_join(j)
        x_done(j)
        norm_rows(j)
    if W < 2:
        relay(wo, 0)
        relay(wg, 0)
    seg_col = column(v.SG[0])
    for j in range(W):
        seg_row = jnp.broadcast_to(v.SG[j].astype(f32), (R, R))
        if j == 0:
            seg_row = jnp.where(lower, seg_row, v.SG[W].astype(f32))
        v.BIAS[:, pl.ds(j * R, R)] = jnp.where(seg_col == seg_row, 0.0, -1e30)
    relayed(wq)
    lane_head = lax.broadcasted_iota(jnp.int32, (R, HC), 1) // HEAD_DIM

    def by_heads(ref, val):
        for h in range(H):
            ref[pl.ds(h * R, R), :] = jnp.where(lane_head == h, val, 0.0).astype(bf16)

    def from_heads(ref, other):
        mix = jnp.zeros((R, HC), f32)
        for h in range(H):
            part = jnp.dot(ref[pl.ds(h * R, R), :], other[...], preferred_element_type=f32)
            mix = jnp.where(lane_head == h, part, mix)
        return mix

    by_heads(
        v.QH,
        jnp.dot(v.N1[pl.ds(0, R), :], v.WQKV[:, pl.ds(0, HC)], preferred_element_type=f32),
    )
    relayed(wk)
    relayed(wv)
    for dst, col in ((v.KB, HC), (v.VB, 2 * HC)):
        dst[...] = jnp.dot(
            v.N1[...], v.WQKV[:, pl.ds(col, HC)], preferred_element_type=f32
        ).astype(bf16)
    relay(wg, 1)

    AR = 64 if R % 64 == 0 else R // 4
    WR = W * R

    def merged(i):
        at, inner = rows(i * AR, AR), rows(lax.rem(i, R // AR) * AR, AR)
        place = lax.broadcasted_iota(jnp.int32, (AR, R), 0) + lax.rem(i, R // AR) * AR
        low = lax.broadcasted_iota(jnp.int32, (AR, R), 1) <= place
        first = jnp.where(low, v.S[at, pl.ds(0, R)], v.S[at, pl.ds(WR, R)])
        if W > 1:
            first = jnp.concatenate([first, v.S[at, pl.ds(R, WR - R)]], axis=1)
        return first, at, inner, low

    def spread(ref, at, low, val):
        own = val[:, :R]
        ref[at, pl.ds(0, R)] = jnp.where(low, own, 0.0).astype(bf16)
        ref[at, pl.ds(WR, R)] = jnp.where(low, 0.0, own).astype(bf16)
        if W > 1:
            ref[at, pl.ds(R, WR - R)] = val[:, R:].astype(bf16)

    def soft(i, _):
        s, at, inner, low = merged(i)
        s = s * (HEAD_DIM**-0.5) + v.BIAS[inner, :]
        e = jnp.exp(s - jnp.max(s, axis=-1, keepdims=True))
        prob = e * (1.0 / jnp.sum(e, axis=-1, keepdims=True))
        v.PM[at, :] = prob
        spread(v.PB, at, low, prob)
        return 0

    for h in range(H):
        v.S[pl.ds(h * R, R), :] = contract(v.QH[pl.ds(h * R, R), :], v.KB[...], (1, 1))
    relay(wu, 0)
    lax.fori_loop(0, H * R // AR, soft, 0)
    v.OB[...] = from_heads(v.PB, v.VB).astype(bf16)

    def chunk(i):
        return pl.ds(i * RC, RC)

    def sum_begin(a, product):
        s1, r1, s2, r2 = v.S1.at[a], v.R1.at[a], v.S2.at[a], v.R2.at[a]
        s1[...] = product((1 - core) * HF).astype(bf16)
        first, second = outgoing(s1), outgoing(s2)
        for i in range(NCHK):
            send(s1.at[chunk(i)], r1.at[chunk(i)], base.a + a * NCHK + i, to_core, None, first)
        v.P32[...] = product(core * HF)
        for i in range(NCHK):
            got(r1.at[chunk(i)], base.a + a * NCHK + i)
            s2[chunk(i), :] = (v.P32[chunk(i), :] + r1[chunk(i), :].astype(f32)).astype(bf16)
            send(s2.at[chunk(i)], r2.at[chunk(i)], base.b + a * NCHK + i, to_y, None, second)

    def sum_end(a, i):
        s2, r2 = v.S2.at[a], v.R2.at[a]
        got(r2.at[chunk(i)], base.b + a * NCHK + i)
        return s2[chunk(i), :].astype(f32) + r2[chunk(i), :].astype(f32)

    def my_rows(i):
        return rows(core * HF + i * RC, RC)

    def their_rows(i):
        return rows((1 - core) * HF + i * RC, RC)

    def share(ref, flow, i):
        if i == 0:
            relays[flow] = outgoing(ref.at[own_half])
        send(ref.at[my_rows(i)], ref.at[my_rows(i)], flow + i, to_core, None, relays[flow])

    def shared(ref, flow):
        for i in range(NCHK):
            got(ref.at[their_rows(i)], flow + i)

    relayed(wo)
    sum_begin(
        0,
        lambda off: jnp.dot(v.OB[rows(off, HF), :], v.WO[...], preferred_element_type=f32),
    )
    relay(wu, 1)
    for i in range(NCHK):
        h_now = v.XB[my_rows(i), :].astype(f32) + sum_end(0, i)
        v.H[chunk(i), :] = h_now
        r = lax.rsqrt(jnp.mean(h_now * h_now, axis=-1, keepdims=True) + EPS)
        v.N2[my_rows(i), :] = (h_now * r * v.gain_two[...]).astype(bf16)
        share(v.N2, base.n2, i)
    relay(wd, 0)
    relay(wd, 1)
    shared(v.N2, base.n2)

    relayed(wg)
    v.GB[...] = contract(v.N2[...], v.WG[...], (1, 1)).astype(bf16)
    relayed(wu)
    v.UB[...] = contract(v.N2[...], v.WU[...], (1, 1)).astype(bf16)

    def activate(i, _):
        at = rows(i * RC, RC)
        g, u = v.GB[at, :].astype(f32), v.UB[at, :].astype(f32)
        v.AB[at, :] = (g / (1.0 + jnp.exp(-g)) * u).astype(bf16)
        return 0

    lax.fori_loop(0, R // RC, activate, 0)
    relayed(wd)
    sum_begin(
        1,
        lambda off: jnp.dot(v.AB[rows(off, HF), :], v.WD[...], preferred_element_type=f32),
    )
    te_copy.wait()
    up_copy.wait()
    squares, counted = jnp.zeros((1, 1), f32), jnp.zeros((1, 1), f32)
    for i in range(NCHK):
        y_now = v.H[chunk(i), :] + sum_end(1, i)
        v.YB[my_rows(i), :] = y_now.astype(bf16)
        weighting = v.VC[my_rows(i), pl.ds(0, 1)]
        differ = y_now - v.TE[chunk(i), :].astype(f32)
        squares = squares + total_of(weighting * differ * differ)
        counted = counted + total_of(weighting)
        dy = v.UP[chunk(i), :].astype(f32) + weighting * differ
        v.DY[chunk(i), :] = dy
        v.DYB[my_rows(i), :] = dy.astype(bf16)
        share(v.DYB, base.dy, i)
    tile_row = lax.broadcasted_iota(jnp.int32, (8, 128), 0)
    v.LT[0] = jnp.where(
        tile_row == 0, jnp.broadcast_to(squares, (8, 128)), jnp.broadcast_to(counted, (8, 128))
    )
    send(v.LT.at[0], v.LT.at[1], base.lc, to_core)
    y_half = v.YB.at[own_half]
    send(y_half, y_half, base.yb, to_core)
    grads_out = [outgoing(v.XS.at[owner(d)]) for d in range(1, F)]
    group_in, group_out = outgoing(v.XS.at[fs]), outgoing(v.GRAD, jnp.logical_not(is_outer))
    shared(v.DYB, base.dy)

    sent, own_done = [0], [0]

    def weight_grad(left, right, at, d, flipped=False):
        who = owner(d)
        tokens = left.shape[1 if flipped else 0]
        n = left.shape[0 if flipped else 1]
        if d == 0:
            own_done[0] = at + n
        rhs = right[pl.ds(0, tokens), pl.ds(hint(who * DF, 128), DF)]
        v.XS[who, pl.ds(at, n), :] = contract(left[...], rhs, (1 if flipped else 0, 0)).astype(bf16)

    def grad_index(d, j):
        return base.gx + (d - 1) * (NCH + 1) + j

    def grad_send(d, at, j):
        rcopy(
            v.XS.at[owner(d), at], v.XR.at[d - 1, at], grads_out[d - 1], grad_index(d, j),
            {"fsdp": owner(d)},
        ).start()

    def grads_ready(upto):
        first, last = sent[0], upto // CH
        sent[0] = last

        def body(j, _):
            for d in range(1, F):
                grad_send(d, rows(j * CH, CH), j)
            return 0

        if last > first:
            lax.fori_loop(first, last, body, 0)

    def inward(at, j):
        for d in range(1, F):
            got(v.XR.at[d - 1, at], grad_index(d, j))
        acc = v.XS[fs, at, :].astype(f32)
        for d in range(1, F):
            acc = acc + v.XR[d - 1, at, :].astype(f32)
        v.XS[fs, at, :] = acc.astype(bf16)

        @pl.when(jnp.logical_not(is_outer))
        def _():
            got(v.ZO.at[at], base.zo + j)
            v.XS[fs, at, :] = (acc + v.ZO[at, :].astype(f32)).astype(bf16)

        @pl.when(is_mid)
        def _():
            rcopy(v.XS.at[fs, at], v.ZI.at[at], group_in, base.zi + j, to_inner).start()

        @pl.when(jnp.logical_not(is_mid))
        def _():
            rcopy(v.XS.at[fs, at], v.ZO.at[at], group_in, base.zo + j, to_inner).start()

    def outward(at, j):
        got(v.ZI.at[at], base.zi + j)

        @pl.when(is_mid)
        def _():
            whole = v.XS[fs, at, :].astype(f32) + v.ZI[at, :].astype(f32)
            v.GRAD[at, :] = whole.astype(bf16)

        @pl.when(jnp.logical_not(is_mid))
        def _():
            v.GRAD[at, :] = v.ZI[at, :]

        @pl.when(jnp.logical_not(is_outer))
        def _():
            rcopy(v.GRAD.at[at], v.ZI.at[at], group_out, base.zi + j, to_outer).start()

        pltpu.make_async_copy(v.GRAD.at[at], v.grad_out.at[at], ls.at[10]).start()

    lag_in, lag_out = SKEW * hop, SKEW * (2 * half - 1 - hop)
    LAST = NCH + SKEW * (2 * half - 1)

    def pump(first, last):
        def body(i, _):
            ja, jb = i - lag_in, i - lag_out
            pl.when((ja >= 0) & (ja < NCH))(lambda: inward(rows(ja * CH, CH), ja))
            pl.when((jb >= 0) & (jb < NCH))(lambda: outward(rows(jb * CH, CH), jb))
            return 0

        if last > first:
            lax.fori_loop(first, last, body, 0)

    pumped = [0]

    def pump_to(last):
        ready = min(sent[0], own_done[0] // CH)
        last = min(last if NCH > 40 else last * NCH // 49, ready if ready < NCH else LAST)
        if last > pumped[0]:
            pump(pumped[0], last)
            pumped[0] = last

    peers = range(1, F)
    for d in peers:
        weight_grad(v.AB, v.DYB, 0, d)
    grads_ready(FF)
    v.S[pl.ds(0, R), pl.ds(0, FF)] = contract(v.DYB[...], v.WD[...], (1, 1))

    def activate_back(i, _):
        at = rows(i * RC, RC)
        g, u, da = v.GB[at, :].astype(f32), v.UB[at, :].astype(f32), v.S[at, pl.ds(0, FF)]
        sig = 1.0 / (1.0 + jnp.exp(-g))
        v.DGB[at, :] = (da * u * (sig * (1.0 + g * (1.0 - sig)))).astype(bf16)
        v.DUB[at, :] = (da * (g * sig)).astype(bf16)
        return 0

    lax.fori_loop(0, R // RC, activate_back, 0)
    sum_begin(
        2,
        lambda off: jnp.dot(v.DGB[rows(off, HF), :], v.WG[...], preferred_element_type=f32)
        + jnp.dot(v.DUB[rows(off, HF), :], v.WU[...], preferred_element_type=f32),
    )
    weight_grad(v.AB, v.DYB, 0, 0)
    for d in peers:
        weight_grad(v.DGB, v.N2, FF, d)
    grads_ready(2 * FF)
    for d in peers:
        weight_grad(v.DUB, v.N2, 2 * FF, d)
    grads_ready(3 * FF)
    weight_grad(v.DGB, v.N2, FF, 0)
    weight_grad(v.DUB, v.N2, 2 * FF, 0)
    pump_to(2)
    v.GT[0] = jnp.zeros((8, D), f32)
    for i in range(NCHK):
        dn2 = sum_end(2, i)
        h_now = v.H[chunk(i), :]
        r = lax.rsqrt(jnp.mean(h_now * h_now, axis=-1, keepdims=True) + EPS)
        gd = v.gain_two[...] * dn2
        dh = v.DY[chunk(i), :] + r * gd - h_now * (
            r * r * r * jnp.mean(gd * h_now, axis=-1, keepdims=True)
        )
        v.DH[chunk(i), :] = dh
        v.DHB[my_rows(i), :] = dh.astype(bf16)
        share(v.DHB, base.dh, i)
        part = jnp.sum(dn2 * h_now * r, axis=0, keepdims=True)
        part = jnp.where(yy == i // (NCHK // 2), part, 0.0)
        v.GT[0, pl.ds(0, 1), :] = v.GT[0, pl.ds(0, 1), :] + part
        pump_to(3 + i)
    shared(v.DHB, base.dh)

    by_heads(v.DOH, contract(v.DHB[...], v.WO[...], (1, 1)))
    pump_to(7)
    for h in range(H):
        v.S[pl.ds(h * R, R), :] = contract(v.DOH[pl.ds(h * R, R), :], v.VB[...], (1, 1))
    for d in peers:
        weight_grad(v.OB, v.DHB, 3 * FF, d)
    grads_ready(3 * FF + HC)
    weight_grad(v.OB, v.DHB, 3 * FF, 0)
    pump_to(8)

    def soft_back(i, _):
        dp, at, _, low = merged(i)
        prob = v.PM[at, :]
        spread(v.DSB, at, low, prob * (dp - jnp.sum(prob * dp, axis=-1, keepdims=True)))
        return 0

    lax.fori_loop(0, H * R // AR, soft_back, 0)
    pump_to(9)
    scale = HEAD_DIM**-0.5
    v.DVT[...] = contract(v.DOH[...], v.PB[...], (0, 0)).astype(bf16)
    v.DKT[...] = (contract(v.QH[...], v.DSB[...], (0, 0)) * scale).astype(bf16)
    v.DQ[...] = (from_heads(v.DSB, v.KB) * scale).astype(bf16)
    pump_to(11)

    def dn1_product(j, which):
        at = pl.ds(hint(j * R + which * HF, 128), HF)
        out = contract(v.DKT[:, at], v.WQKV[:, pl.ds(HC, HC)], (0, 1))
        out = out + contract(v.DVT[:, at], v.WQKV[:, pl.ds(2 * HC, HC)], (0, 1))
        if j == 0:
            out = out + contract(v.DQ[rows(which * HF, HF), :], v.WQKV[:, pl.ds(0, HC)], (1, 1))
        return out

    for j in range(W, -1, -1):
        v.D1S[j] = dn1_product(j, 1 - core).astype(bf16)
        send(v.D1S.at[j], v.D1R.at[j], base.d1 + j, to_core)
        v.D1O[j] = dn1_product(j, core)
    for d in list(peers) + [0]:
        at = 3 * FF + HC
        weight_grad(v.DQ, v.N1, at, d)
        weight_grad(v.DKT, v.N1, at + HC, d, True)
        weight_grad(v.DVT, v.N1, at + 2 * HC, d, True)
        if d == F - 1:
            grads_ready(N)
    pump_to(13)
    for j in range(W, -1, -1):
        got(v.D1R.at[j], base.d1 + j)
        there = rows((1 - yy) * Q, Q)
        v.D2S[j] = (v.D1O[j, there, :] + v.D1R[j, there, :].astype(f32)).astype(bf16)
        send(v.D2S.at[j], v.D2R.at[j], base.d2 + j, to_y)
    pump_to(16)
    here = rows(yy * Q, Q)
    for j in range(W, 0, -1):
        got(v.D2R.at[j], base.d2 + j)
        own = v.D1O[j, here, :] + v.D1R[j, here, :].astype(f32) + v.D2R[j].astype(f32)
        v.DZS[j] = own.astype(bf16)
        if j < W:
            @pl.when(has_next & (z >= j))
            def _(j=j, own=own):
                got(v.DZR.at[j + 1], base.dz + j + 1)
                v.DZS[j] = (own + v.DZR[j + 1].astype(f32)).astype(bf16)
        send(v.DZS.at[j], v.DZR.at[j], base.dz + j, to_prev, z >= j)
        pump_to(19 + 2 * (W - j))

    got(v.LT.at[1], base.lc)
    v.LB[z] = v.LT[0] + v.LT[1]
    for s in range(C - 1):
        left_tile, right_tile = z - s, z + s
        send(v.LB.at[jnp.maximum(left_tile, 0)], v.LB.at[jnp.maximum(left_tile, 0)],
             base.lr + s, to_next, has_next & (left_tile >= 0))
        send(v.LB.at[jnp.minimum(right_tile, C - 1)], v.LB.at[jnp.minimum(right_tile, C - 1)],
             base.ll + s, to_prev, has_prev & (right_tile <= C - 1))
        if s == 0:
            pump_to(23)
        pl.when(left_tile - 1 >= 0)(
            lambda i=left_tile - 1, s=s: got(v.LB.at[jnp.maximum(i, 0)], base.lr + s)
        )
        pl.when(right_tile + 1 <= C - 1)(
            lambda i=right_tile + 1, s=s: got(v.LB.at[jnp.minimum(i, C - 1)], base.ll + s)
        )
    v.LX[fs] = v.LB[...]
    for d in peers:
        send(v.LB, v.LX.at[fs], base.lx + d - 1, {"fsdp": owner(d)})

    pump_to(26)
    got(v.D2R.at[0], base.d2)
    v.P32[pl.ds(0, Q), :] = (
        v.D1O[0, here, :] + v.D1R[0, here, :].astype(f32) + v.D2R[0].astype(f32)
    )

    @pl.when(has_next)
    def _():
        got(v.DZR.at[1], base.dz + 1)
        v.P32[pl.ds(0, Q), :] = v.P32[pl.ds(0, Q), :] + v.DZR[1].astype(f32)

    quarter = rows(core * HF + yy * Q, Q)
    dn1 = v.P32[pl.ds(0, Q), :]
    x_now = v.XB[quarter, :].astype(f32)
    r = lax.rsqrt(jnp.mean(x_now * x_now, axis=-1, keepdims=True) + EPS)
    gd = v.gain_one[...] * dn1
    gi = v.DH[here, :] + r * gd - x_now * (
        r * r * r * jnp.mean(gd * x_now, axis=-1, keepdims=True)
    )
    v.GIB[quarter, :] = gi.astype(bf16)
    mine = v.GIB.at[quarter]
    send(mine, mine, base.i1, to_y)
    send(mine, mine, base.i2, to_core)
    v.GT[0, pl.ds(1, 1), :] = jnp.sum(dn1 * x_now * r, axis=0, keepdims=True)
    send(v.GT.at[0], v.GR.at[0], base.g1, to_core)
    pump_to(28)
    got(v.GR.at[0], base.g1)
    v.GT[1] = v.GT[0] + v.GR[0]
    send(v.GT.at[1], v.GR.at[1], base.g2, to_y)
    from_y = v.GIB.at[rows(core * HF + (1 - yy) * Q, Q)]
    got(from_y, base.i1)
    send(from_y, from_y, base.i3, to_core)
    pump_to(32)
    got(v.GR.at[1], base.g2)
    v.GT[2] = v.GT[1] + v.GR[1]
    for d in list(peers) + [0]:
        tile = v.GT[2, :, pl.ds(hint(owner(d) * DF, 128), DF)]
        v.XS[owner(d), pl.ds(N, 16), :] = jnp.concatenate([tile, jnp.zeros_like(tile)], 0).astype(bf16)
        if d:
            grad_send(d, pl.ds(N, 16), NCH)

    for d in peers:
        got(v.LX.at[owner(F - d)], base.lx + d - 1)
    sums = [sum(v.LX[s, c] for c in range(C)) for s in range(F)]
    counted = sum(s[1:2, :] for s in sums)
    for s in range(F):
        v.LOSS[pl.ds(s, 1), :] = sums[s][0:1, :] * F / (counted * D)

    pump_to(LAST - SKEW * (2 * half - 1))
    gain_rows = pl.ds(N, 16)
    inward(gain_rows, NCH)
    pump_to(LAST)
    outward(gain_rows, NCH)
    got(v.YB.at[rows((1 - core) * HF, HF)], base.yb)
    got(v.GIB.at[rows((1 - core) * HF + yy * Q, Q)], base.i2)
    got(v.GIB.at[rows((1 - core) * HF + (1 - yy) * Q, Q)], base.i3)
    results = (
        pltpu.make_async_copy(v.YB, v.y_out, ls.at[0]),
        pltpu.make_async_copy(v.GIB, v.gi_out, ls.at[1]),
        pltpu.make_async_copy(v.LOSS, v.loss_out, ls.at[2]),
    )
    for cp in results:
        cp.start()

    for k, (src, cond) in enumerate(unsent):
        def left(src=src, k=k):
            rcopy(src, src, k, 0, to_core).wait_send()
        if cond is None:
            left()
        else:
            pl.when(cond)(left)
    for cp in results:
        cp.wait()
    pltpu.make_async_copy(v.GRAD, v.grad_out, ls.at[10]).wait()


def finish_kernel(p, grad, gib, yb, loss, *refs):
    (y_out, loss_out, gi_out, one, gq, gk, gv, go, two, gg, gu, gd) = refs[:12]
    g_buf, i_buf, y_buf, l_buf, g_wide, i_wide, q_wide, sem_in, sem_out = refs[12:]
    FF, HC, N = p.FF, p.HC, p.N
    at = 3 * FF
    plain, flip = [], []
    for ref, first in ((gd, 0), (gg, FF), (gu, 2 * FF)):
        plain += [(ref, first, 0, FF // 2), (ref, first + FF // 2, FF // 2, FF // 2)]
    plain.append((go, at, 0, HC))
    flip = [(gq, at + HC), (gk, at + 2 * HC), (gv, at + 3 * HC)]
    loads = []

    def load(src, dst):
        cp = pltpu.make_async_copy(src, dst, sem_in.at[len(loads)])
        cp.start()
        loads.append(cp)
        return cp

    stores = []

    def store(src, dst):
        cp = pltpu.make_async_copy(src, dst, sem_out.at[len(stores)])
        cp.start()
        stores.append(cp)

    plain_in = [load(grad.at[pl.ds(f, n)], g_buf.at[pl.ds(f, n)]) for _, f, _, n in plain]
    flip_in = [load(grad.at[pl.ds(f, HC)], g_buf.at[pl.ds(f, HC)]) for _, f in flip]
    gi_in = load(gib, i_buf)
    y_in = load(yb, y_buf)
    gain_in = load(grad.at[pl.ds(N, 16)], g_buf.at[pl.ds(N, 16)])
    loss_in = load(loss, l_buf)
    for (ref, first, row, n), cp in zip(plain, plain_in):
        cp.wait()
        g_wide[pl.ds(first, n), :] = g_buf[pl.ds(first, n), :].astype(f32)
        store(g_wide.at[pl.ds(first, n)], ref.at[pl.ds(row, n)])
    for k, ((ref, first), cp) in enumerate(zip(flip, flip_in)):
        cp.wait()
        for c in range(0, HC, 128):
            w = min(128, HC - c)
            q_wide[k, :, pl.ds(c, w)] = g_buf[pl.ds(first + c, w), :].astype(f32).T
        store(q_wide.at[k], ref)
    gi_in.wait()
    i_wide[...] = i_buf[...].astype(f32)
    store(i_wide, gi_out.at[0])
    y_in.wait()
    store(y_buf, y_out.at[0])
    gain_in.wait()
    gains = g_buf[pl.ds(N, 16), :].astype(f32)
    two[...] = gains[0:1, :]
    one[...] = gains[1:2, :]
    loss_in.wait()
    for s in range(p.F):
        loss_out[s] = jnp.max(l_buf[pl.ds(s, 1), :])
    for cp in stores:
        cp.wait()


def shards(mesh_shape, seq_len, *args):
    (inputs, upstream, teacher, valid, segment, gain_one, wq, wk, wv, wo, gain_two, wg, wu, wd) = args
    _, rows_here, width = inputs.shape
    p = Plan(
        mesh_shape["fsdp"], mesh_shape["ctx"], rows_here, width, wq.shape[1], wg.shape[1], seq_len
    )
    R, D, DF, HC, FF, F = p.R, p.D, p.DF, p.HC, p.FF, p.F
    NG = p.N + 16
    scratch = scratch_of(p)
    vmem = pl.BlockSpec(memory_space=pltpu.VMEM)
    anywhere = pl.BlockSpec(memory_space=pl.ANY)
    in_specs = [anywhere] * 3 + [vmem] * 3 + [anywhere] * 4 + [vmem] + [anywhere] * 3
    sds = jax.ShapeDtypeStruct
    grad, gib, yb, loss = pl.pallas_call(
        functools.partial(layer_kernel, p, tuple(scratch)),
        out_shape=(
            sds((NG, DF), bf16), sds((R, D), bf16), sds((R, D), bf16), sds((max(F, 8), 128), f32),
        ),
        in_specs=in_specs,
        out_specs=(anywhere,) * 4,
        scratch_shapes=[pltpu.VMEM(s, dt) for s, dt in scratch.values()]
        + [
            pltpu.SemaphoreType.DMA((p.sends,)), pltpu.SemaphoreType.DMA((p.total,)),
            pltpu.SemaphoreType.DMA((11,)),
        ],
        compiler_params=pltpu.CompilerParams(
            collective_id=0, has_side_effects=True, vmem_limit_bytes=67043328
        ),
        name="layer",
    )(
        inputs.reshape(R, D), upstream.reshape(R, D), teacher.reshape(R, D), valid, segment,
        gain_one.reshape(1, D), wq, wk, wv, wo, gain_two.reshape(1, D), wg.T, wu.T, wd,
    )
    outs = pl.pallas_call(
        functools.partial(finish_kernel, p),
        out_shape=(
            sds((1, R, D), bf16), sds((F,), f32), sds((1, R, D), f32), sds((1, DF), f32),
            sds((DF, HC), f32), sds((DF, HC), f32), sds((DF, HC), f32), sds((HC, DF), f32),
            sds((1, DF), f32), sds((FF, DF), f32), sds((FF, DF), f32), sds((FF, DF), f32),
        ),
        in_specs=[anywhere] * 4,
        out_specs=(anywhere, pl.BlockSpec(memory_space=pltpu.SMEM), anywhere, vmem)
        + (anywhere,) * 4 + (vmem,) + (anywhere,) * 3,
        scratch_shapes=[
            pltpu.VMEM((NG, DF), bf16), pltpu.VMEM((R, D), bf16), pltpu.VMEM((R, D), bf16),
            pltpu.VMEM((max(F, 8), 128), f32), pltpu.VMEM((3 * FF + HC, DF), f32),
            pltpu.VMEM((R, D), f32), pltpu.VMEM((3, DF, HC), f32),
            pltpu.SemaphoreType.DMA((14,)), pltpu.SemaphoreType.DMA((12,)),
        ],
        compiler_params=pltpu.CompilerParams(vmem_limit_bytes=40 * 2**20),
        name="finish",
    )(grad, gib, yb, loss)
    outs = list(outs)
    outs[3], outs[8] = outs[3].reshape(DF), outs[8].reshape(DF)
    outs[9], outs[10] = outs[9].T, outs[10].T
    return tuple(outs)


def solution(mesh):
    def run(*args):
        token, row, col = P("fsdp", "ctx", None), P("fsdp", "tp"), P("tp", "fsdp")
        pair = P("fsdp", "ctx")
        return jax.shard_map(
            functools.partial(shards, dict(mesh.shape), args[0].shape[1]),
            mesh=mesh,
            in_specs=(token, token, token, pair, pair, P(), row, row, row, col, P(), row, row, col),
            out_specs=(
                token, P(), token, P("fsdp"), row, row, row, col, P("fsdp"), row, row, col,
            ),
            check_vma=False,
        )(*args)

    return run
```

time: 201 us -> 184 us (0.915)
  Pallas kernels: 189 us -> 178 us
  local copies, waits for them, and re-layouts: 11.3 us -> 4.66 us
    pallas_call x1, Pallas kernels: 186 us -> 173 us  [shards(): pl.pallas_call(functools.partial(layer_kernel, p, tuple(scratch)), out_sh...]
    unnamed x14 -> x8, local copies, waits for them, and re-layouts: 11.3 us -> 4.66 us
    pallas_call x1, Pallas kernels: 2.9 us -> 5.06 us  [shards(): pl.pallas_call(functools.partial(finish_kernel, p), out_shape=(sds((1, R,...]
where the time goes in v2:
time: 184 us
  Pallas kernels  178 us (97%)
  local copies, waits for them, and re-layouts  4.66 us (3%)
    pallas_call x1, Pallas kernels, shards(): pl.pallas_call(functools.partial(layer_kernel, p, tuple(scratch)), out_sh...  173 us
    pallas_call x1, Pallas kernels, shards(): pl.pallas_call(functools.partial(finish_kernel, p), out_shape=(sds((1, R,...  5.06 us
    unnamed x8, local copies, waits for them, and re-layouts  4.66 us

profile of v2, /device:TPU:0, one launch (start us, length us, event | category | flops | bytes accessed | tf_op | source)
XLA Modules:
  0.0 183.5 jit_solution(2677862934329557172)
XLA Ops:
  0.6 173.0 %layer.1 = (bf16[3152,512]{1,0:T(8,128)(2,1)}, bf16[256,1024]{1,0:T(8,128)(2,1)}, bf16[256,1024]{1,0:T(8,128)(2,1)}, f32[8,128]{1,0:T(8,128)}) custom-call(bf16[256,1024]{1,0:T(8,128)(2,1)} %bitcast.13, bf16[256,1024]{1,0:T(8,128)(2,1)} %bitcast.14, bf16[256,1024]{1,0:T(8,128)(2,1)} %bitcast.15, s32[1,256]{1,0:T(1,128)} %refs_3_.1, s32[1,256]{1,0:T(1,128)} %refs_4_.1, ...), custom_call_target="tpu_custom_call" | custom-call | tf_op jit(solution)/shard_map/layer/pallas_call | solution.py:827
  173.7 0.0 copy-start
  173.7 1.9 %copy-done = bf16[3152,512]{1,0:T(8,128)(2,1)S(1)} copy-done((bf16[3152,512]{1,0:T(8,128)(2,1)S(1)}, bf16[3152,512]{1,0:T(8,128)(2,1)}, u32[]{:S(2)}) %copy-start) | copy-done | bytes 3227672
  175.6 0.0 copy-start.1
  175.6 1.0 copy-done.1
  176.6 0.0 copy-start.2
  176.6 1.0 copy-done.2
  177.6 0.0 copy-start.3
  177.7 0.7 copy-done.3
  178.3 5.1 %finish.1 = (bf16[1,256,1024]{2,1,0:T(8,128)(2,1)}, f32[2]{0:T(128)}, f32[1,256,1024]{2,1,0:T(8,128)}, f32[1,512]{1,0:T(1,128)}, f32[512,256]{1,0:T(8,128)}, /*i...) custom-call(bf16[3152,512]{1,0:T(8,128)(2,1)S(1)} %copy-done, ...), custom_call_target="tpu_custom_call" | custom-call | tf_op jit(solution)/shard_map/finish/pallas_call | solution.py:847
Async XLA Ops:
  173.7 1.9 %copy-start = (bf16[3152,512]{1,0:T(8,128)(2,1)S(1)}, bf16[3152,512]{1,0:T(8,128)(2,1)}, u32[]{:S(2)}) copy-start(bf16[3152,512]{1,0:T(8,128)(2,1)} %get-tuple-element.28.grad) | copy-start | bytes 9682948
  175.6 1.0 copy-start.1
  176.6 1.0 copy-start.2
  177.6 0.7 copy-start.3

commit v3 on v2

--- a/solution.py
+++ b/solution.py
@@ -12,7 +12,7 @@
 EPS = 1e-05
 MESH = pl.DeviceIdType.MESH
 NCHK = 4
-SKEW = 3
+SKEW = 2
 f32, bf16 = jnp.float32, jnp.bfloat16
 
 
@@ -24,7 +24,7 @@
         self.W = -(-(seq_len // 2) // rows)
         self.N = 3 * hidden + 4 * head_cols
         self.CH = next(
-            k for k in range(16, self.N + 1, 16) if self.N % k == 0 and k * self.DF >= 32768
+            k for k in range(16, self.N + 1, 16) if self.N % k == 0 and k * self.DF >= 57344
         )
         self.NCH = self.N // self.CH
         self.base, self.total = SimpleNamespace(), 0
@@ -32,7 +32,7 @@
         for name, count in dict(
             xz=self.W, sg=self.W, xy=self.W, xc=self.W, wd=10 * peers, wr=10 * peers,
             a=3 * NCHK, b=3 * NCHK, n2=NCHK, yb=1, dy=NCHK, dh=NCHK,
-            lc=1, lr=ctx, ll=ctx, lx=peers, d1=self.W + 1, d2=self.W + 1, dz=self.W + 1,
+            lc=1, ll=ctx - 1, lx=peers, d1=self.W + 1, d2=self.W + 1, dz=self.W + 1,
             g1=1, g2=1, i1=1, i2=1, i3=1, gx=peers * (self.NCH + 1),
             zo=self.NCH + 1, zi=self.NCH + 1,
         ).items():
@@ -70,7 +70,7 @@
         D2S=((W + 1, Q, D), bf16), D2R=((W + 1, Q, D), bf16), DZR=((W + 1, Q, D), bf16),
         DZS=((W + 1, Q, D), bf16),
         GT=((3, 8, D), f32), GR=((2, 8, D), f32),
-        LT=((2, 8, 128), f32), LB=((C, 8, 128), f32), LX=((F, C, 8, 128), f32),
+        LT=((8, 128), f32), LX=((F, 8, 128), f32), LC=((F, 8, 128), f32), LB=((C, F, 8, 128), f32),
         XS=((F, NG, DF), bf16), XR=((F - 1, NG, DF), bf16),
         ZO=((NG, DF), bf16), ZI=((NG, DF), bf16), GRAD=((NG, DF), bf16), GIB=((R, D), bf16),
         YB=((R, D), bf16), LOSS=((max(F, 8), 128), f32),
@@ -187,11 +187,9 @@
     greet(to_y)
     for d in range(1, F):
         greet({"fsdp": owner(d)})
-    pl.when(has_next)(lambda: greet(to_next))
-    pl.when(has_prev)(lambda: greet(to_prev))
-    pl.semaphore_wait(
-        barrier, 2 + F - 1 + has_next.astype(jnp.int32) + has_prev.astype(jnp.int32)
-    )
+    for k in range(1, C):
+        greet({"ctx": lax.rem(z + k, C)})
+    pl.semaphore_wait(barrier, F + C)
 
     def piece_index(kind, number, d):
         return kind + number * (F - 1) + d - 1
@@ -444,10 +442,13 @@
         v.DYB[my_rows(i), :] = dy.astype(bf16)
         share(v.DYB, base.dy, i)
     tile_row = lax.broadcasted_iota(jnp.int32, (8, 128), 0)
-    v.LT[0] = jnp.where(
+    tile = jnp.where(
         tile_row == 0, jnp.broadcast_to(squares, (8, 128)), jnp.broadcast_to(counted, (8, 128))
     )
-    send(v.LT.at[0], v.LT.at[1], base.lc, to_core)
+    v.LT[...] = tile
+    v.LX[fs] = tile
+    for d in range(1, F):
+        send(v.LT, v.LX.at[fs], base.lx + d - 1, {"fsdp": owner(d)})
     y_half = v.YB.at[own_half]
     send(y_half, y_half, base.yb, to_core)
     grads_out = [outgoing(v.XS.at[owner(d)]) for d in range(1, F)]
@@ -540,9 +541,10 @@
 
     pumped = [0]
 
-    def pump_to(last):
+    def pump_to(place):
+        last = LAST if place > 49 else place * NCH // 49
         ready = min(sent[0], own_done[0] // CH)
-        last = min(last if NCH > 40 else last * NCH // 49, ready if ready < NCH else LAST)
+        last = min(last, ready if ready < NCH else LAST)
         if last > pumped[0]:
             pump(pumped[0], last)
             pumped[0] = last
@@ -568,6 +570,9 @@
         + jnp.dot(v.DUB[rows(off, HF), :], v.WU[...], preferred_element_type=f32),
     )
     weight_grad(v.AB, v.DYB, 0, 0)
+    for d in peers:
+        got(v.LX.at[owner(F - d)], base.lx + d - 1)
+    send(v.LX, v.LC, base.lc, to_core)
     for d in peers:
         weight_grad(v.DGB, v.N2, FF, d)
     grads_ready(2 * FF)
@@ -594,6 +599,10 @@
         v.GT[0, pl.ds(0, 1), :] = v.GT[0, pl.ds(0, 1), :] + part
         pump_to(3 + i)
     shared(v.DHB, base.dh)
+    got(v.LC, base.lc)
+    v.LB[z] = v.LX[...] + v.LC[...]
+    for k in range(1, C):
+        send(v.LB.at[z], v.LB.at[z], base.ll + k - 1, {"ctx": lax.rem(z + k, C)})
 
     by_heads(v.DOH, contract(v.DHB[...], v.WO[...], (1, 1)))
     pump_to(7)
@@ -658,26 +667,7 @@
         send(v.DZS.at[j], v.DZR.at[j], base.dz + j, to_prev, z >= j)
         pump_to(19 + 2 * (W - j))
 
-    got(v.LT.at[1], base.lc)
-    v.LB[z] = v.LT[0] + v.LT[1]
-    for s in range(C - 1):
-        left_tile, right_tile = z - s, z + s
-        send(v.LB.at[jnp.maximum(left_tile, 0)], v.LB.at[jnp.maximum(left_tile, 0)],
-             base.lr + s, to_next, has_next & (left_tile >= 0))
-        send(v.LB.at[jnp.minimum(right_tile, C - 1)], v.LB.at[jnp.minimum(right_tile, C - 1)],
-             base.ll + s, to_prev, has_prev & (right_tile <= C - 1))
-        if s == 0:
-            pump_to(23)
-        pl.when(left_tile - 1 >= 0)(
-            lambda i=left_tile - 1, s=s: got(v.LB.at[jnp.maximum(i, 0)], base.lr + s)
-        )
-        pl.when(right_tile + 1 <= C - 1)(
-            lambda i=right_tile + 1, s=s: got(v.LB.at[jnp.minimum(i, C - 1)], base.ll + s)
-        )
-    v.LX[fs] = v.LB[...]
-    for d in peers:
-        send(v.LB, v.LX.at[fs], base.lx + d - 1, {"fsdp": owner(d)})
-
+    pump_to(23)
     pump_to(26)
     got(v.D2R.at[0], base.d2)
     v.P32[pl.ds(0, Q), :] = (
@@ -719,18 +709,17 @@
         if d:
             grad_send(d, pl.ds(N, 16), NCH)
 
-    for d in peers:
-        got(v.LX.at[owner(F - d)], base.lx + d - 1)
-    sums = [sum(v.LX[s, c] for c in range(C)) for s in range(F)]
+    pump_to(49)
+    gain_rows = pl.ds(N, 16)
+    inward(gain_rows, NCH)
+    pump_to(50)
+    outward(gain_rows, NCH)
+    for k in range(1, C):
+        got(v.LB.at[lax.rem(z + C - k, C)], base.ll + k - 1)
+    sums = [sum(v.LB[c, s] for c in range(C)) for s in range(F)]
     counted = sum(s[1:2, :] for s in sums)
     for s in range(F):
         v.LOSS[pl.ds(s, 1), :] = sums[s][0:1, :] * F / (counted * D)
-
-    pump_to(LAST - SKEW * (2 * half - 1))
-    gain_rows = pl.ds(N, 16)
-    inward(gain_rows, NCH)
-    pump_to(LAST)
-    outward(gain_rows, NCH)
     got(v.YB.at[rows((1 - core) * HF, HF)], base.yb)
     got(v.GIB.at[rows((1 - core) * HF + yy * Q, Q)], base.i2)
     got(v.GIB.at[rows((1 - core) * HF + (1 - yy) * Q, Q)], base.i3)

time: 184 us -> 172 us (0.935)
  Pallas kernels: 178 us -> 166 us
    pallas_call x1, Pallas kernels: 173 us -> 161 us  [shards(): pl.pallas_call(functools.partial(layer_kernel, p, tuple(scratch)), out_sh...]
where the time goes in v3:
time: 172 us; the launch traced here: 171 us
  Pallas kernels  166 us (97%)
  local copies, waits for them, and re-layouts  4.66 us (3%)
    pallas_call x1, Pallas kernels, shards(): pl.pallas_call(functools.partial(layer_kernel, p, tuple(scratch)), out_sh...  161 us
    pallas_call x1, Pallas kernels, shards(): pl.pallas_call(functools.partial(finish_kernel, p), out_shape=(sds((1, R,...  5.06 us
    unnamed x8, local copies, waits for them, and re-layouts  4.66 us

profile of v3, /device:TPU:0, one launch (start us, length us, event | category | flops | bytes accessed | tf_op | source)
XLA Modules:
  0.0 171.4 jit_solution(10928682365762658281)
XLA Ops:
  0.6 160.8 %layer.1 = (bf16[3152,512]{1,0:T(8,128)(2,1)}, bf16[256,1024]{1,0:T(8,128)(2,1)}, bf16[256,1024]{1,0:T(8,128)(2,1)}, f32[8,128]{1,0:T(8,128)}) custom-call(bf16[256,1024]{1,0:T(8,128)(2,1)} %bitcast.13, bf16[256,1024]{1,0:T(8,128)(2,1)} %bitcast.14, bf16[256,1024]{1,0:T(8,128)(2,1)} %bitcast.15, s32[1,256]{1,0:T(1,128)} %refs_3_.1, s32[1,256]{1,0:T(1,128)} %refs_4_.1, ...), custom_call_target="tpu_custom_call" | custom-call | tf_op jit(solution)/shard_map/layer/pallas_call | solution.py:816
  161.5 0.0 copy-start
  161.5 1.9 %copy-done = bf16[3152,512]{1,0:T(8,128)(2,1)S(1)} copy-done((bf16[3152,512]{1,0:T(8,128)(2,1)S(1)}, bf16[3152,512]{1,0:T(8,128)(2,1)}, u32[]{:S(2)}) %copy-start) | copy-done | bytes 3227672
  163.4 0.0 copy-start.1
  163.4 1.0 copy-done.1
  164.4 0.0 copy-start.2
  164.4 1.0 copy-done.2
  165.5 0.0 copy-start.3
  165.5 0.7 copy-done.3
  166.1 5.1 %finish.1 = (bf16[1,256,1024]{2,1,0:T(8,128)(2,1)}, f32[2]{0:T(128)}, f32[1,256,1024]{2,1,0:T(8,128)}, f32[1,512]{1,0:T(1,128)}, f32[512,256]{1,0:T(8,128)}, /*i...) custom-call(bf16[3152,512]{1,0:T(8,128)(2,1)S(1)} %copy-done, ...), custom_call_target="tpu_custom_call" | custom-call | tf_op jit(solution)/shard_map/finish/pallas_call | solution.py:836
Async XLA Ops:
  161.5 1.9 %copy-start = (bf16[3152,512]{1,0:T(8,128)(2,1)S(1)}, bf16[3152,512]{1,0:T(8,128)(2,1)}, u32[]{:S(2)}) copy-start(bf16[3152,512]{1,0:T(8,128)(2,1)} %get-tuple-element.28.grad) | copy-start | bytes 9682948
  163.4 1.0 copy-start.1
  164.4 1.0 copy-start.2
  165.5 0.7 copy-start.3

commit v4 on v3

--- a/solution.py
+++ b/solution.py
@@ -12,6 +12,7 @@
 EPS = 1e-05
 MESH = pl.DeviceIdType.MESH
 NCHK = 4
+YROWS = 2
 SKEW = 2
 f32, bf16 = jnp.float32, jnp.bfloat16
 
@@ -30,8 +31,8 @@
         self.base, self.total = SimpleNamespace(), 0
         peers = fsdp - 1
         for name, count in dict(
-            xz=self.W, sg=self.W, xy=self.W, xc=self.W, wd=10 * peers, wr=10 * peers,
-            a=3 * NCHK, b=3 * NCHK, n2=NCHK, yb=1, dy=NCHK, dh=NCHK,
+            ya=YROWS * fsdp, ys=YROWS * fsdp, xz=self.W, sg=self.W, xy=self.W, xc=self.W, wd=11 * peers, wr=11 * peers,
+            a=3 * NCHK, b=3 * NCHK, n2=NCHK, yb=1, dy=YROWS * fsdp, dh=NCHK,
             lc=1, ll=ctx - 1, lx=peers, d1=self.W + 1, d2=self.W + 1, dz=self.W + 1,
             g1=1, g2=1, i1=1, i2=1, i3=1, gx=peers * (self.NCH + 1),
             zo=self.NCH + 1, zi=self.NCH + 1,
@@ -137,47 +138,6 @@
     def rows(off, n, m=16):
         return pl.ds(hint(off, m), n)
 
-    local = []
-
-    def fetch(src, dst):
-        cp = pltpu.make_async_copy(src, dst, ls.at[len(local)])
-        cp.start()
-        local.append(cp)
-        return cp
-
-    own_half = rows(core * HF, HF)
-    x_copy = fetch(v.x, v.XB.at[pl.ds(0, R)])
-    own_cols = pl.ds(hint(fs * DF, 128), DF)
-
-    def by_row(dst, col0, cols):
-        def region(who, off, n):
-            return dst.at[rows(who * DF + off, n), pl.ds(col0, cols)]
-        return region
-
-    def by_col(dst):
-        def region(who, off, n):
-            return dst.at[rows(off, n), pl.ds(hint(who * DF, 128), DF)]
-        return region
-
-    weights = (
-        (v.wq, by_row(v.WQKV, 0, HC), 1), (v.wk, by_row(v.WQKV, HC, HC), 1),
-        (v.wv, by_row(v.WQKV, 2 * HC, HC), 1), (v.wo, by_col(v.WO), 1),
-        (v.wg, by_col(v.WG), 2), (v.wu, by_col(v.WU), 2), (v.wd, by_col(v.WD), 2),
-    )
-    gathers = []
-    count = 0
-    for source, region, parts in weights:
-        tall = source.shape[0]
-        cut = tall // 2 // parts
-        gathers.append((
-            source, fetch(source, region(fs, 0, tall)),
-            [(region, tall // 2, k * cut, cut, count + k) for k in range(parts)],
-        ))
-        count += parts
-    wq, wk, wv, wo, wg, wu, wd = gathers
-    te_copy = fetch(v.teacher.at[own_half], v.TE)
-    up_copy = fetch(v.upstream.at[own_half], v.UP)
-
     barrier = pltpu.get_barrier_semaphore()
 
     def greet(dev):
@@ -189,6 +149,50 @@
         greet({"fsdp": owner(d)})
     for k in range(1, C):
         greet({"ctx": lax.rem(z + k, C)})
+
+    local = []
+
+    def fetch(src, dst):
+        cp = pltpu.make_async_copy(src, dst, ls.at[len(local)])
+        cp.start()
+        local.append(cp)
+        return cp
+
+    own_half = rows(core * HF, HF)
+    x_copy = fetch(v.x, v.XB.at[pl.ds(0, R)])
+    own_cols = pl.ds(hint(fs * DF, 128), DF)
+
+    def by_row(dst, col0, cols):
+        def region(who, off, n):
+            return dst.at[rows(who * DF + off, n), pl.ds(col0, cols)]
+        return region
+
+    def by_col(dst):
+        def region(who, off, n):
+            return dst.at[rows(off, n), pl.ds(hint(who * DF, 128), DF)]
+        return region
+
+    weights = (
+        (v.wq, by_row(v.WQKV, 0, HC), 1), (v.wk, by_row(v.WQKV, HC, HC), 1),
+        (v.wv, by_row(v.WQKV, 2 * HC, HC), 1), (v.wo, by_col(v.WO), 1),
+        (v.wg, by_col(v.WG), 2), (v.wu, by_col(v.WU), 2), (v.wd, by_col(v.WD), 3),
+    )
+    gathers = []
+    count = 0
+    for source, region, parts in weights:
+        tall = source.shape[0]
+        cuts = [0, tall // 2]
+        for _ in range(parts - 1):
+            cuts.insert(-1, (cuts[-2] + cuts[-1] + 31) // 32 * 16)
+        gathers.append((
+            source, fetch(source, region(fs, 0, tall)),
+            [(region, tall // 2, cuts[k], cuts[k + 1] - cuts[k], count + k) for k in range(parts)],
+        ))
+        count += parts
+    wq, wk, wv, wo, wg, wu, wd = gathers
+    te_copy = fetch(v.teacher.at[own_half], v.TE)
+    up_copy = fetch(v.upstream.at[own_half], v.UP)
+
     pl.semaphore_wait(barrier, F + C)
 
     def piece_index(kind, number, d):
@@ -218,8 +222,9 @@
                 part, part, piece_index(base.wr, number, d), to_pair, None, relays[number - which, d]
             )
 
-    def relayed(weight):
-        weight[1].wait()
+    def relayed(weight, with_own=True):
+        if with_own:
+            weight[1].wait()
         for region, tall, at, n, number in weight[2]:
             for d in range(1, F):
                 got(region(owner(F - d), (1 - par) * tall + at, n), piece_index(base.wr, number, d))
@@ -279,20 +284,16 @@
     x_pass(1)
     relay(wk, 0)
     relay(wv, 0)
-    x_join(1)
-    x_done(1)
-    norm_rows(1)
-    for j in range(2, W + 1):
-        x_pass(j)
-        if j == 2:
+    for j in range(1, W + 1):
+        if j < W:
+            x_pass(j + 1)
+        x_join(j)
+        if j == 1:
             relay(wo, 0)
+        if j == W:
             relay(wg, 0)
-        x_join(j)
         x_done(j)
         norm_rows(j)
-    if W < 2:
-        relay(wo, 0)
-        relay(wg, 0)
     seg_col = column(v.SG[0])
     for j in range(W):
         seg_row = jnp.broadcast_to(v.SG[j].astype(f32), (R, R))
@@ -400,14 +401,16 @@
         lambda off: jnp.dot(v.OB[rows(off, HF), :], v.WO[...], preferred_element_type=f32),
     )
     relay(wu, 1)
+    relay(wd, 0)
     for i in range(NCHK):
         h_now = v.XB[my_rows(i), :].astype(f32) + sum_end(0, i)
         v.H[chunk(i), :] = h_now
         r = lax.rsqrt(jnp.mean(h_now * h_now, axis=-1, keepdims=True) + EPS)
         v.N2[my_rows(i), :] = (h_now * r * v.gain_two[...]).astype(bf16)
         share(v.N2, base.n2, i)
-    relay(wd, 0)
-    relay(wd, 1)
+        if i == 1:
+            relay(wd, 1)
+    relay(wd, 2)
     shared(v.N2, base.n2)
 
     relayed(wg)
@@ -422,25 +425,56 @@
         return 0
 
     lax.fori_loop(0, R // RC, activate, 0)
-    relayed(wd)
-    sum_begin(
-        1,
-        lambda off: jnp.dot(v.AB[rows(off, HF), :], v.WD[...], preferred_element_type=f32),
-    )
+    YR = HF // YROWS
+    s1, r1, s2, r2 = v.S1.at[1], v.R1.at[1], v.S2.at[1], v.R2.at[1]
+    first, second, to_share = outgoing(s1), outgoing(s2), outgoing(v.DYB.at[own_half])
+
+    def col_block(d):
+        return pl.ds(hint(owner(d) * DF, 128), DF)
+
+    def y_parts(d):
+        return [(d * YROWS + k, k * YR) for k in range(YROWS)]
+
+    def y_begin(d):
+        cols = col_block(d)
+        s1[:, cols] = jnp.dot(
+            v.AB[rows((1 - core) * HF, HF), :], v.WD[:, cols], preferred_element_type=f32
+        ).astype(bf16)
+        for i, off in y_parts(d):
+            at = s1.at[pl.ds(off, YR), cols]
+            send(at, r1.at[pl.ds(off, YR), cols], base.ya + i, to_core, None, first)
+        v.P32[:, cols] = jnp.dot(v.AB[own_half, :], v.WD[:, cols], preferred_element_type=f32)
+        for i, off in y_parts(d):
+            part = pl.ds(off, YR)
+            got(r1.at[part, cols], base.ya + i)
+            s2[part, cols] = (v.P32[part, cols] + r1[part, cols].astype(f32)).astype(bf16)
+            send(s2.at[part, cols], r2.at[part, cols], base.ys + i, to_y, None, second)
+
+    wd[1].wait()
+    y_begin(0)
+    relayed(wd, False)
+    for d in range(1, F):
+        y_begin(d)
     te_copy.wait()
     up_copy.wait()
     squares, counted = jnp.zeros((1, 1), f32), jnp.zeros((1, 1), f32)
-    for i in range(NCHK):
-        y_now = v.H[chunk(i), :] + sum_end(1, i)
-        v.YB[my_rows(i), :] = y_now.astype(bf16)
-        weighting = v.VC[my_rows(i), pl.ds(0, 1)]
-        differ = y_now - v.TE[chunk(i), :].astype(f32)
-        squares = squares + total_of(weighting * differ * differ)
-        counted = counted + total_of(weighting)
-        dy = v.UP[chunk(i), :].astype(f32) + weighting * differ
-        v.DY[chunk(i), :] = dy
-        v.DYB[my_rows(i), :] = dy.astype(bf16)
-        share(v.DYB, base.dy, i)
+    for d in range(F):
+        cols = col_block(d)
+        for i, off in y_parts(d):
+            part, mine = pl.ds(off, YR), rows(core * HF + off, YR)
+            got(r2.at[part, cols], base.ys + i)
+            y_now = v.H[part, cols] + s2[part, cols].astype(f32) + r2[part, cols].astype(f32)
+            v.YB[mine, cols] = y_now.astype(bf16)
+            weighting = v.VC[mine, pl.ds(0, 1)]
+            differ = y_now - v.TE[part, cols].astype(f32)
+            squares = squares + total_of(weighting * differ * differ)
+            if d == 0:
+                counted = counted + total_of(weighting)
+            dy = v.UP[part, cols].astype(f32) + weighting * differ
+            v.DY[part, cols] = dy
+            v.DYB[mine, cols] = dy.astype(bf16)
+            at = v.DYB.at[mine, cols]
+            send(at, at, base.dy + i, to_core, None, to_share)
     tile_row = lax.broadcasted_iota(jnp.int32, (8, 128), 0)
     tile = jnp.where(
         tile_row == 0, jnp.broadcast_to(squares, (8, 128)), jnp.broadcast_to(counted, (8, 128))
@@ -453,7 +487,9 @@
     send(y_half, y_half, base.yb, to_core)
     grads_out = [outgoing(v.XS.at[owner(d)]) for d in range(1, F)]
     group_in, group_out = outgoing(v.XS.at[fs]), outgoing(v.GRAD, jnp.logical_not(is_outer))
-    shared(v.DYB, base.dy)
+    for d in range(F):
+        for i, off in y_parts(d):
+            got(v.DYB.at[rows((1 - core) * HF + off, YR), col_block(d)], base.dy + i)
 
     sent, own_done = [0], [0]
 
@@ -712,8 +748,6 @@
     pump_to(49)
     gain_rows = pl.ds(N, 16)
     inward(gain_rows, NCH)
-    pump_to(50)
-    outward(gain_rows, NCH)
     for k in range(1, C):
         got(v.LB.at[lax.rem(z + C - k, C)], base.ll + k - 1)
     sums = [sum(v.LB[c, s] for c in range(C)) for s in range(F)]
@@ -731,13 +765,26 @@
     for cp in results:
         cp.start()
 
-    for k, (src, cond) in enumerate(unsent):
-        def left(src=src, k=k):
+    streams = grads_out + [group_in, group_out]
+
+    def all_left(k):
+        src, cond = unsent[k]
+
+        def left():
             rcopy(src, src, k, 0, to_core).wait_send()
+
         if cond is None:
             left()
         else:
             pl.when(cond)(left)
+
+    for k in range(len(unsent)):
+        if k not in streams:
+            all_left(k)
+    pump_to(50)
+    outward(gain_rows, NCH)
+    for k in streams:
+        all_left(k)
     for cp in results:
         cp.wait()
     pltpu.make_async_copy(v.GRAD, v.grad_out, ls.at[10]).wait()
@@ -849,7 +896,7 @@
             pltpu.VMEM((R, D), f32), pltpu.VMEM((3, DF, HC), f32),
             pltpu.SemaphoreType.DMA((14,)), pltpu.SemaphoreType.DMA((12,)),
         ],
-        compiler_params=pltpu.CompilerParams(vmem_limit_bytes=40 * 2**20),
+        compiler_params=pltpu.CompilerParams(vmem_limit_bytes=67043328),
         name="finish",
     )(grad, gib, yb, loss)
     outs = list(outs)

time: 172 us -> 161 us (0.936)
  Pallas kernels: 166 us -> 160 us
  local copies, waits for them, and re-layouts: 4.66 us -> 0 us
    pallas_call x1, Pallas kernels: 161 us -> 155 us  [shards(): pl.pallas_call(functools.partial(layer_kernel, p, tuple(scratch)), out_sh...]
    unnamed x8 -> x0, local copies, waits for them, and re-layouts: 4.66 us -> none
where the time goes in v4:
time: 161 us
  Pallas kernels  160 us (99%)
    pallas_call x1, Pallas kernels, shards(): pl.pallas_call(functools.partial(layer_kernel, p, tuple(scratch)), out_sh...  155 us
    pallas_call x1, Pallas kernels, shards(): pl.pallas_call(functools.partial(finish_kernel, p), out_shape=(sds((1, R,...  5.02 us

profile of v4, /device:TPU:0, one launch (start us, length us, event | category | flops | bytes accessed | tf_op | source)
XLA Modules:
  0.0 160.7 jit_solution(6878106466901467856)
XLA Ops:
  0.6 154.9 %layer.1 = (bf16[3152,512]{1,0:T(8,128)(2,1)}, bf16[256,1024]{1,0:T(8,128)(2,1)}, bf16[256,1024]{1,0:T(8,128)(2,1)}, f32[8,128]{1,0:T(8,128)}) custom-call(bf16[256,1024]{1,0:T(8,128)(2,1)} %bitcast.13, bf16[256,1024]{1,0:T(8,128)(2,1)} %bitcast.14, bf16[256,1024]{1,0:T(8,128)(2,1)} %bitcast.15, s32[1,256]{1,0:T(1,128)} %refs_3_.1, s32[1,256]{1,0:T(1,128)} %refs_4_.1, ...), custom_call_target="tpu_custom_call" | custom-call | tf_op jit(solution)/shard_map/layer/pallas_call | solution.py:863
  155.6 5.0 %finish.1 = (bf16[1,256,1024]{2,1,0:T(8,128)(2,1)}, f32[2]{0:T(128)}, f32[1,256,1024]{2,1,0:T(8,128)}, f32[1,512]{1,0:T(1,128)}, f32[512,256]{1,0:T(8,128)}, /*i...) custom-call(bf16[3152,512]{1,0:T(8,128)(2,1)} %get-tuple-element.28., ...), custom_call_target="tpu_custom_call" | custom-call | tf_op jit(solution)/shard_map/finish/pallas_call | solution.py:883

commit v5 on v4

--- a/solution.py
+++ b/solution.py
@@ -31,7 +31,7 @@
         self.base, self.total = SimpleNamespace(), 0
         peers = fsdp - 1
         for name, count in dict(
-            ya=YROWS * fsdp, ys=YROWS * fsdp, xz=self.W, sg=self.W, xy=self.W, xc=self.W, wd=11 * peers, wr=11 * peers,
+            ya=YROWS * fsdp, ys=YROWS * fsdp, xz=2 * self.W, sg=self.W, xy=2 * self.W, xc=self.W, wd=11 * peers, wr=11 * peers,
             a=3 * NCHK, b=3 * NCHK, n2=NCHK, yb=1, dy=YROWS * fsdp, dh=NCHK,
             lc=1, ll=ctx - 1, lx=peers, d1=self.W + 1, d2=self.W + 1, dz=self.W + 1,
             g1=1, g2=1, i1=1, i2=1, i3=1, gx=peers * (self.NCH + 1),
@@ -181,12 +181,15 @@
     count = 0
     for source, region, parts in weights:
         tall = source.shape[0]
-        cuts = [0, tall // 2]
-        for _ in range(parts - 1):
-            cuts.insert(-1, (cuts[-2] + cuts[-1] + 31) // 32 * 16)
+        cuts = [0, tall // 2] if parts == 1 else [0, tall // 4, tall // 2]
+        if parts == 3:
+            cuts.insert(2, tall // 3 // 16 * 16)
         gathers.append((
             source, fetch(source, region(fs, 0, tall)),
-            [(region, tall // 2, cuts[k], cuts[k + 1] - cuts[k], count + k) for k in range(parts)],
+            [
+                (region, cuts[min(parts, 2)], tall // 2, cuts[k], cuts[k + 1] - cuts[k], count + k)
+                for k in range(parts)
+            ],
         ))
         count += parts
     wq, wk, wv, wo, wg, wu, wd = gathers
@@ -202,20 +205,26 @@
         tall = source.shape[0] // 2
         for d in range(1, F):
             group = outgoing(source.at[rows(par * tall, tall)])
-            for region, _, at, n, number in pieces:
+            for region, passed, _, at, n, number in pieces:
                 off = par * tall + at
                 send(
                     source.at[rows(off, n)], region(fs, off, n), piece_index(base.wd, number, d),
                     {"fsdp": owner(d)}, None, group,
                 )
+                if at >= passed:
+                    off = (1 - par) * tall + at
+                    send(
+                        source.at[rows(off, n)], region(fs, off, n),
+                        piece_index(base.wr, number, d), {"fsdp": owner(d)},
+                    )
 
     relays = {}
 
     def relay(weight, which):
-        region, tall, at, n, number = weight[2][which]
+        region, passed, tall, at, n, number = weight[2][which]
         for d in range(1, F):
             if which == 0:
-                relays[number, d] = outgoing(region(owner(F - d), par * tall, tall))
+                relays[number, d] = outgoing(region(owner(F - d), par * tall, passed))
             part = region(owner(F - d), par * tall + at, n)
             got(part, piece_index(base.wd, number, d))
             send(
@@ -225,17 +234,27 @@
     def relayed(weight, with_own=True):
         if with_own:
             weight[1].wait()
-        for region, tall, at, n, number in weight[2]:
+        for region, passed, tall, at, n, number in weight[2]:
             for d in range(1, F):
+                if at >= passed:
+                    got(region(owner(F - d), par * tall + at, n), piece_index(base.wd, number, d))
                 got(region(owner(F - d), (1 - par) * tall + at, n), piece_index(base.wr, number, d))
 
     def x_half(j, which):
         return v.XB.at[rows(j * R + which * HF, HF)]
 
+    def x_eighth(j, y, k):
+        return v.XB.at[rows(j * R + core * HF + y * Q + k * (Q // 2), Q // 2)]
+
     def x_quarter(j, y):
         return v.XB.at[rows(j * R + core * HF + y * Q, Q)]
 
-    send(v.x.at[rows(core * HF + yy * Q, Q)], x_quarter(1, yy), base.xz, to_next, has_next)
+    x_group = outgoing(x_quarter(0, yy), has_next)
+    for k in range(2):
+        send(
+            v.x.at[rows(core * HF + yy * Q + k * (Q // 2), Q // 2)], x_eighth(1, yy, k), base.xz + k,
+            to_next, has_next, x_group,
+        )
     v.SG[0] = v.segment[...]
     send(v.segment, v.SG.at[1], base.sg, to_next, has_next)
     for j in range(1, W + 1):
@@ -245,18 +264,24 @@
             v.SG[j] = jnp.full((1, R), -1, jnp.int32)
 
     def x_pass(j):
-        @pl.when(z >= j)
-        def _():
-            got(x_quarter(j, yy), base.xz + j - 1)
-            got(v.SG.at[j], base.sg + j - 1)
+        both = (z >= j) & has_next
+        onward = outgoing(x_quarter(j, yy), both) if j < W else None
+        across = outgoing(x_quarter(j, yy), z >= j)
+        for k in range(2):
+            part = x_eighth(j, yy, k)
+            pl.when(z >= j)(lambda part=part, k=k: got(part, base.xz + 2 * (j - 1) + k))
+            if j < W:
+                send(part, x_eighth(j + 1, yy, k), base.xz + 2 * j + k, to_next, both, onward)
+            send(part, part, base.xy + 2 * (j - 1) + k, to_y, z >= j, across)
+        pl.when(z >= j)(lambda: got(v.SG.at[j], base.sg + j - 1))
         if j < W:
-            both = (z >= j) & has_next
-            send(x_quarter(j, yy), x_quarter(j + 1, yy), base.xz + j, to_next, both)
             send(v.SG.at[j], v.SG.at[j + 1], base.sg + j, to_next, both)
-        send(x_quarter(j, yy), x_quarter(j, yy), base.xy + j - 1, to_y, z >= j)
 
     def x_join(j):
-        pl.when(z >= j)(lambda: got(x_quarter(j, 1 - yy), base.xy + j - 1))
+        for k in range(2):
+            pl.when(z >= j)(
+                lambda k=k: got(x_eighth(j, 1 - yy, k), base.xy + 2 * (j - 1) + k)
+            )
         send(x_half(j, core), x_half(j, core), base.xc + j - 1, to_core, z >= j)
 
     def x_done(j):
@@ -280,8 +305,8 @@
     x_copy.wait()
     norm_rows(0)
     v.VC[...] = jnp.broadcast_to(column(v.valid[...]), (R, 128))
+    x_pass(1)
     relay(wq, 0)
-    x_pass(1)
     relay(wk, 0)
     relay(wv, 0)
     for j in range(1, W + 1):
@@ -356,8 +381,8 @@
 
     for h in range(H):
         v.S[pl.ds(h * R, R), :] = contract(v.QH[pl.ds(h * R, R), :], v.KB[...], (1, 1))
+    lax.fori_loop(0, H * R // AR, soft, 0)
     relay(wu, 0)
-    lax.fori_loop(0, H * R // AR, soft, 0)
     v.OB[...] = from_heads(v.PB, v.VB).astype(bf16)
 
     def chunk(i):
@@ -410,7 +435,6 @@
         share(v.N2, base.n2, i)
         if i == 1:
             relay(wd, 1)
-    relay(wd, 2)
     shared(v.N2, base.n2)
 
     relayed(wg)
@@ -444,6 +468,9 @@
             at = s1.at[pl.ds(off, YR), cols]
             send(at, r1.at[pl.ds(off, YR), cols], base.ya + i, to_core, None, first)
         v.P32[:, cols] = jnp.dot(v.AB[own_half, :], v.WD[:, cols], preferred_element_type=f32)
+
+    def y_pass(d):
+        cols = col_block(d)
         for i, off in y_parts(d):
             part = pl.ds(off, YR)
             got(r1.at[part, cols], base.ya + i)
@@ -455,6 +482,8 @@
     relayed(wd, False)
     for d in range(1, F):
         y_begin(d)
+    for d in range(F):
+        y_pass(d)
     te_copy.wait()
     up_copy.wait()
     squares, counted = jnp.zeros((1, 1), f32), jnp.zeros((1, 1), f32)

time: 161 us -> 158 us (0.981)
  Pallas kernels: 160 us -> 157 us
    pallas_call x1, Pallas kernels: 155 us -> 152 us  [shards(): pl.pallas_call(functools.partial(layer_kernel, p, tuple(scratch)), out_sh...]
where the time goes in v5:
time: 158 us
  Pallas kernels  157 us (99%)
    pallas_call x1, Pallas kernels, shards(): pl.pallas_call(functools.partial(layer_kernel, p, tuple(scratch)), out_sh...  152 us
    pallas_call x1, Pallas kernels, shards(): pl.pallas_call(functools.partial(finish_kernel, p), out_shape=(sds((1, R,...  5.02 us

profile of v5, /device:TPU:0, one launch (start us, length us, event | category | flops | bytes accessed | tf_op | source)
XLA Modules:
  0.0 157.7 jit_solution(3025907681359510509)
XLA Ops:
  0.6 151.9 %layer.1 = (bf16[3152,512]{1,0:T(8,128)(2,1)}, bf16[256,1024]{1,0:T(8,128)(2,1)}, bf16[256,1024]{1,0:T(8,128)(2,1)}, f32[8,128]{1,0:T(8,128)}) custom-call(bf16[256,1024]{1,0:T(8,128)(2,1)} %bitcast.13, bf16[256,1024]{1,0:T(8,128)(2,1)} %bitcast.14, bf16[256,1024]{1,0:T(8,128)(2,1)} %bitcast.15, s32[1,256]{1,0:T(1,128)} %refs_3_.1, s32[1,256]{1,0:T(1,128)} %refs_4_.1, ...), custom_call_target="tpu_custom_call" | custom-call | tf_op jit(solution)/shard_map/layer/pallas_call | solution.py:892
  152.5 5.0 %finish.1 = (bf16[1,256,1024]{2,1,0:T(8,128)(2,1)}, f32[2]{0:T(128)}, f32[1,256,1024]{2,1,0:T(8,128)}, f32[1,512]{1,0:T(1,128)}, f32[512,256]{1,0:T(8,128)}, /*i...) custom-call(bf16[3152,512]{1,0:T(8,128)(2,1)} %get-tuple-element.28., ...), custom_call_target="tpu_custom_call" | custom-call | tf_op jit(solution)/shard_map/finish/pallas_call | solution.py:912

commit v6 on v5

--- a/solution.py
+++ b/solution.py
@@ -28,14 +28,17 @@
             k for k in range(16, self.N + 1, 16) if self.N % k == 0 and k * self.DF >= 57344
         )
         self.NCH = self.N // self.CH
+        self.NB = self.NCH - max(1, 224 // self.CH)
+        rest = self.N + 16 - self.NB * self.CH
+        self.CS = next(k for k in (48, 64, 80, 32, 16) if rest % k == 0)
+        self.NK = self.NB + rest // self.CS
         self.base, self.total = SimpleNamespace(), 0
         peers = fsdp - 1
         for name, count in dict(
             ya=YROWS * fsdp, ys=YROWS * fsdp, xz=2 * self.W, sg=self.W, xy=2 * self.W, xc=self.W, wd=11 * peers, wr=11 * peers,
             a=3 * NCHK, b=3 * NCHK, n2=NCHK, yb=1, dy=YROWS * fsdp, dh=NCHK,
             lc=1, ll=ctx - 1, lx=peers, d1=self.W + 1, d2=self.W + 1, dz=self.W + 1,
-            g1=1, g2=1, i1=1, i2=1, i3=1, gx=peers * (self.NCH + 1),
-            zo=self.NCH + 1, zi=self.NCH + 1,
+            g1=1, g2=1, i1=1, i2=1, i3=1, gx=peers * self.NK, zo=self.NK, zi=self.NK,
         ).items():
             setattr(self.base, name, self.total)
             self.total += count
@@ -86,8 +89,8 @@
         v.gain_two, v.wg, v.wu, v.wd, v.grad_out, v.gi_out, v.y_out, v.loss_out,
     ) = refs[:18]
     ss, rs, ls = refs[-3:]
-    R, D, HC, FF, DF, F, C, W, N, CH, NCH = (
-        p.R, p.D, p.HC, p.FF, p.DF, p.F, p.C, p.W, p.N, p.CH, p.NCH
+    R, D, HC, FF, DF, F, C, W, N, CH, NCH, CS, NB, NK = (
+        p.R, p.D, p.HC, p.FF, p.DF, p.F, p.C, p.W, p.N, p.CH, p.NCH, p.CS, p.NB, p.NK
     )
     HF, Q, KR, H = R // 2, R // 4, (W + 1) * R, HC // HEAD_DIM
     RC = HF // NCHK
@@ -532,7 +535,7 @@
         v.XS[who, pl.ds(at, n), :] = contract(left[...], rhs, (1 if flipped else 0, 0)).astype(bf16)
 
     def grad_index(d, j):
-        return base.gx + (d - 1) * (NCH + 1) + j
+        return base.gx + (d - 1) * NK + j
 
     def grad_send(d, at, j):
         rcopy(
@@ -541,7 +544,7 @@
         ).start()
 
     def grads_ready(upto):
-        first, last = sent[0], upto // CH
+        first, last = sent[0], min(upto // CH, NB)
         sent[0] = last
 
         def body(j, _):
@@ -551,6 +554,13 @@
 
         if last > first:
             lax.fori_loop(first, last, body, 0)
+        if upto == N:
+            for j in range(NB, NK - 1):
+                for d in range(1, F):
+                    grad_send(d, small(j), j)
+
+    def small(j):
+        return rows(NB * CH + (j - NB) * CS, CS)
 
     def inward(at, j):
         for d in range(1, F):
@@ -592,13 +602,17 @@
         pltpu.make_async_copy(v.GRAD.at[at], v.grad_out.at[at], ls.at[10]).start()
 
     lag_in, lag_out = SKEW * hop, SKEW * (2 * half - 1 - hop)
-    LAST = NCH + SKEW * (2 * half - 1)
+    LAST = NK + SKEW * (2 * half - 1)
 
     def pump(first, last):
         def body(i, _):
             ja, jb = i - lag_in, i - lag_out
-            pl.when((ja >= 0) & (ja < NCH))(lambda: inward(rows(ja * CH, CH), ja))
-            pl.when((jb >= 0) & (jb < NCH))(lambda: outward(rows(jb * CH, CH), jb))
+            pl.when((ja >= 0) & (ja < NB))(lambda: inward(rows(ja * CH, CH), ja))
+            if last > NB:
+                pl.when((ja >= NB) & (ja < NK))(lambda: inward(small(ja), ja))
+            pl.when((jb >= 0) & (jb < NB))(lambda: outward(rows(jb * CH, CH), jb))
+            if last > NB:
+                pl.when((jb >= NB) & (jb < NK))(lambda: outward(small(jb), jb))
             return 0
 
         if last > first:
@@ -608,8 +622,8 @@
 
     def pump_to(place):
         last = LAST if place > 49 else place * NCH // 49
-        ready = min(sent[0], own_done[0] // CH)
-        last = min(last, ready if ready < NCH else LAST)
+        if place <= 49:
+            last = min(last, sent[0], own_done[0] // CH)
         if last > pumped[0]:
             pump(pumped[0], last)
             pumped[0] = last
@@ -772,11 +786,9 @@
         tile = v.GT[2, :, pl.ds(hint(owner(d) * DF, 128), DF)]
         v.XS[owner(d), pl.ds(N, 16), :] = jnp.concatenate([tile, jnp.zeros_like(tile)], 0).astype(bf16)
         if d:
-            grad_send(d, pl.ds(N, 16), NCH)
+            grad_send(d, small(NK - 1), NK - 1)
 
     pump_to(49)
-    gain_rows = pl.ds(N, 16)
-    inward(gain_rows, NCH)
     for k in range(1, C):
         got(v.LB.at[lax.rem(z + C - k, C)], base.ll + k - 1)
     sums = [sum(v.LB[c, s] for c in range(C)) for s in range(F)]
@@ -811,7 +823,6 @@
         if k not in streams:
             all_left(k)
     pump_to(50)
-    outward(gain_rows, NCH)
     for k in streams:
         all_left(k)
     for cp in results:

time: 158 us -> 157 us (level)
  no operation moved by 1% of the time
where the time goes in v6:
time: 157 us; the launch traced here: 156 us
  Pallas kernels  156 us (99%)
    pallas_call x1, Pallas kernels, shards(): pl.pallas_call(functools.partial(layer_kernel, p, tuple(scratch)), out_sh...  151 us
    pallas_call x1, Pallas kernels, shards(): pl.pallas_call(functools.partial(finish_kernel, p), out_shape=(sds((1, R,...  5.02 us

profile of v6, /device:TPU:0, one launch (start us, length us, event | category | flops | bytes accessed | tf_op | source)
XLA Modules:
  0.0 156.5 jit_solution(7878176430097309508)
XLA Ops:
  0.6 150.7 %layer.1 = (bf16[3152,512]{1,0:T(8,128)(2,1)}, bf16[256,1024]{1,0:T(8,128)(2,1)}, bf16[256,1024]{1,0:T(8,128)(2,1)}, f32[8,128]{1,0:T(8,128)}) custom-call(bf16[256,1024]{1,0:T(8,128)(2,1)} %bitcast.13, bf16[256,1024]{1,0:T(8,128)(2,1)} %bitcast.14, bf16[256,1024]{1,0:T(8,128)(2,1)} %bitcast.15, s32[1,256]{1,0:T(1,128)} %refs_3_.1, s32[1,256]{1,0:T(1,128)} %refs_4_.1, ...), custom_call_target="tpu_custom_call" | custom-call | tf_op jit(solution)/shard_map/layer/pallas_call | solution.py:903
  151.3 5.0 %finish.1 = (bf16[1,256,1024]{2,1,0:T(8,128)(2,1)}, f32[2]{0:T(128)}, f32[1,256,1024]{2,1,0:T(8,128)}, f32[1,512]{1,0:T(1,128)}, f32[512,256]{1,0:T(8,128)}, /*i...) custom-call(bf16[3152,512]{1,0:T(8,128)(2,1)} %get-tuple-element.28., ...), custom_call_target="tpu_custom_call" | custom-call | tf_op jit(solution)/shard_map/finish/pallas_call | solution.py:923

commit v7 on v6

--- a/solution.py
+++ b/solution.py
@@ -438,10 +438,12 @@
         share(v.N2, base.n2, i)
         if i == 1:
             relay(wd, 1)
+
+    relayed(wg)
+    v.GB[own_half, :] = contract(v.N2[own_half, :], v.WG[...], (1, 1)).astype(bf16)
     shared(v.N2, base.n2)
-
-    relayed(wg)
-    v.GB[...] = contract(v.N2[...], v.WG[...], (1, 1)).astype(bf16)
+    other_half = rows((1 - core) * HF, HF)
+    v.GB[other_half, :] = contract(v.N2[other_half, :], v.WG[...], (1, 1)).astype(bf16)
     relayed(wu)
     v.UB[...] = contract(v.N2[...], v.WU[...], (1, 1)).astype(bf16)
 

time: 157 us -> 157 us (level)
  no operation moved by 1% of the time
where the time goes in v7:
time: 157 us; the launch traced here: 156 us
  Pallas kernels  155 us (99%)
    pallas_call x1, Pallas kernels, shards(): pl.pallas_call(functools.partial(layer_kernel, p, tuple(scratch)), out_sh...  150 us
    pallas_call x1, Pallas kernels, shards(): pl.pallas_call(functools.partial(finish_kernel, p), out_shape=(sds((1, R,...  5.02 us

profile of v7, /device:TPU:0, one launch (start us, length us, event | category | flops | bytes accessed | tf_op | source)
XLA Modules:
  0.0 156.3 jit_solution(7106055241323929042)
XLA Ops:
  0.6 150.5 %layer.1 = (bf16[3152,512]{1,0:T(8,128)(2,1)}, bf16[256,1024]{1,0:T(8,128)(2,1)}, bf16[256,1024]{1,0:T(8,128)(2,1)}, f32[8,128]{1,0:T(8,128)}) custom-call(bf16[256,1024]{1,0:T(8,128)(2,1)} %bitcast.13, bf16[256,1024]{1,0:T(8,128)(2,1)} %bitcast.14, bf16[256,1024]{1,0:T(8,128)(2,1)} %bitcast.15, s32[1,256]{1,0:T(1,128)} %refs_3_.1, s32[1,256]{1,0:T(1,128)} %refs_4_.1, ...), custom_call_target="tpu_custom_call" | custom-call | tf_op jit(solution)/shard_map/layer/pallas_call | solution.py:905
  151.1 5.0 %finish.1 = (bf16[1,256,1024]{2,1,0:T(8,128)(2,1)}, f32[2]{0:T(128)}, f32[1,256,1024]{2,1,0:T(8,128)}, f32[1,512]{1,0:T(1,128)}, f32[512,256]{1,0:T(8,128)}, /*i...) custom-call(bf16[3152,512]{1,0:T(8,128)(2,1)} %get-tuple-element.28., ...), custom_call_target="tpu_custom_call" | custom-call | tf_op jit(solution)/shard_map/finish/pallas_call | solution.py:925
